TPU v7x, 32 devices: a whole 2x2x4 slice. The times are simulated.
32 devices in a mesh: dp: 4 (over y, x), fsdp: 8 (over z, core).
Axes of the slice: x: 2, y: 2, z: 4, core: 2. Of those that a mesh axis runs over, the one named last changes fastest.
Arguments:
- tokens: bfloat16 [32768, 1024], P(('dp', 'fsdp')), may hold values from -6 to 6
- cotangent: bfloat16 [32768, 1024], P(('dp', 'fsdp')), may hold values from -15 to 15
- clip_frames: int32 [32, 4], P(('dp', 'fsdp')), may hold values from 0 to 4, as said below
- levels: int32 [128], P(('dp', 'fsdp')), may hold values from 0 to 999
- pad_mask: int32 [32768], P(('dp', 'fsdp')), may hold values from 0 to 1, as said below
- w_mod: bfloat16 [1024, 6144], P(('dp', 'fsdp')), may hold values from -0.1875 to 0.1875
- b_mod: bfloat16 [6144], P(('dp', 'fsdp')), may hold values from -3 to 3
- w_qkv: bfloat16 [1024, 3072], P(('dp', 'fsdp')), may hold values from -0.1875 to 0.1875
- b_qkv: bfloat16 [3072], P(('dp', 'fsdp')), may hold values from -3 to 3
- w_out: bfloat16 [1024, 1024], P(('dp', 'fsdp')), may hold values from -3 to 3
- b_out: bfloat16 [1024], P(('dp', 'fsdp')), may hold values from -3 to 3
- w_up: bfloat16 [1024, 4096], P(('dp', 'fsdp')), may hold values from -0.1875 to 0.1875
- b_up: bfloat16 [4096], P(('dp', 'fsdp')), may hold values from -3 to 3
- w_down: bfloat16 [4096, 1024], P(('dp', 'fsdp')), may hold values from -0.09375 to 0.09375
- b_down: bfloat16 [1024], P(('dp', 'fsdp')), may hold values from -3 to 3
- noise_table: bfloat16 [1024, 1000], P(('dp', 'fsdp')), may hold values from -6 to 6
Outputs:
- block_out: bfloat16 [32768, 1024], P(('dp', 'fsdp'))
- token_grad: bfloat16 [32768, 1024], P(('dp', 'fsdp'))
- wmod_grad: float32 [1024, 6144], P(('dp', 'fsdp'))
- bmod_grad: float32 [6144], P(('dp', 'fsdp'))
- wqkv_grad: float32 [1024, 3072], P(('dp', 'fsdp'))
- bqkv_grad: float32 [3072], P(('dp', 'fsdp'))
- wout_grad: float32 [1024, 1024], P(('dp', 'fsdp'))
- bout_grad: float32 [1024], P(('dp', 'fsdp'))
- wup_grad: float32 [1024, 4096], P(('dp', 'fsdp'))
- bup_grad: float32 [4096], P(('dp', 'fsdp'))
- wdown_grad: float32 [4096, 1024], P(('dp', 'fsdp'))
- bdown_grad: float32 [1024], P(('dp', 'fsdp'))
- table_grad: float32 [1024, 1000], P(('dp', 'fsdp'))
Inputs may be any that keep to these rules, and one draw needn't show every extreme that they name: `clip_frames`: each row sums to 4, its nonzero entries come first; in every draw some device's row is one clip of 4 frames. `pad_mask`: the first of the 256 tokens of every frame is live.
All inputs are finite; a program needn't handle non-finite values.
Results may differ from a plain program's by a relative error of at most 0.013.
The roundings to bfloat16 on the way count: a program that leaves them out, or rounds other values in their place, can miss the bound.
Values may be sent and summed in bfloat16 or wider, within the bound.
A program may use at most 256 MiB of HBM per device.

v0:
```python
import jax
import jax.numpy as jnp
from jax import lax
from jax.sharding import PartitionSpec as P

HD = 64


epsilon = 1e-06
highest = lax.Precision.HIGHEST


def clip_positions(clip_row, patch_size):
    frame_count = clip_row.shape[0]
    slots = jnp.arange(frame_count, dtype=jnp.int32)
    ends = jnp.cumsum(clip_row)
    clip_of = jnp.sum((slots[:, None] >= ends[None, :]).astype(jnp.int32), axis=1)
    starts = ends - clip_row
    start_of = jnp.sum(jnp.where(clip_of[:, None] == slots[None, :], starts[None, :], 0), axis=1)
    frame_of = slots - start_of
    return (jnp.repeat(clip_of, patch_size), jnp.repeat(frame_of, patch_size))


def rotate(values, frame_tok, patch_tok, sign):
    half_dim = values.shape[-1] // 2
    quarter_dim = half_dim // 2
    freq = 10000.0 ** (-jnp.arange(quarter_dim, dtype=jnp.float32) / quarter_dim)
    angle = jnp.concatenate(
        [
            frame_tok.astype(jnp.float32)[:, None] * freq[None, :],
            patch_tok.astype(jnp.float32)[:, None] * freq[None, :],
        ],
        axis=1,
    )
    cosine = jnp.cos(angle)[:, None, :]
    sine = sign * jnp.sin(angle)[:, None, :]
    first = values[..., :half_dim]
    second = values[..., half_dim:]
    return jnp.concatenate(
        [first * cosine - second * sine, second * cosine + first * sine], axis=-1
    )


def normalize(values):
    centred = values - jnp.mean(values, axis=-1, keepdims=True)
    inverse = lax.rsqrt(jnp.mean(centred * centred, axis=-1, keepdims=True) + epsilon)
    return (centred * inverse, inverse)


def normalize_back(grad, normed, inverse):
    return inverse * (
        grad
        - jnp.mean(grad, axis=-1, keepdims=True)
        - normed * jnp.mean(grad * normed, axis=-1, keepdims=True)
    )


def scale_by(values, factor, frame_count):
    shaped = values.reshape(frame_count, -1, values.shape[-1])
    return (shaped * factor[:, None, :]).reshape(values.shape)


def modulate(values, scale, shift, frame_count):
    shaped = values.reshape(frame_count, -1, values.shape[-1])
    return (shaped * (1.0 + scale[:, None, :]) + shift[:, None, :]).reshape(values.shape)


def frame_sum(values, frame_count):
    return jnp.sum(values.reshape(frame_count, -1, values.shape[-1]), axis=1)


def contract_rows(left, right):
    return lax.dot_general(
        left, right, (((0,), (0,)), ((), ())), preferred_element_type=jnp.float32
    )


def contract_cols(left, right):
    return lax.dot_general(
        left, right, (((1,), (1,)), ((), ())), preferred_element_type=jnp.float32
    )


def gelu_slope(values):
    return (
        0.5 * (1.0 + lax.erf(values * 0.7071067811865476))
        + values * jnp.exp(-0.5 * values * values) * 0.3989422804014327
    )


def block_scores(query_block, key_head, allow_block):
    raw = contract_cols(query_block, key_head) * 0.125
    return jnp.where(allow_block, raw, -1e30)


def head_forward(query_head, key_head, value_head, allowed_blocks):

    def one_block(block_items):
        scores = block_scores(block_items[0], key_head, block_items[1])
        top = jnp.max(scores, axis=1, keepdims=True)
        expo = jnp.exp(scores - top)
        total = jnp.sum(expo, axis=1, keepdims=True)
        softmax_w = (expo / total).astype(jnp.bfloat16)
        result = jnp.dot(softmax_w, value_head, preferred_element_type=jnp.float32).astype(
            jnp.bfloat16
        )
        return (result, (top + jnp.log(total))[:, 0])

    return lax.map(one_block, (query_head, allowed_blocks))


def head_backward(query_head, key_head, value_head, grad_head, lse_head, allowed_blocks):

    def one_block(carry, block_items):
        grad_key, grad_value = carry
        query_block, grad_block, lse_block, allow_block = block_items
        scores = block_scores(query_block, key_head, allow_block)
        softmax_f = jnp.exp(scores - lse_block[:, None])
        softmax_w = softmax_f.astype(jnp.bfloat16)
        grad_value = grad_value + contract_rows(softmax_w, grad_block)
        grad_probs = contract_cols(grad_block, value_head)
        delta = jnp.sum(softmax_f * grad_probs, axis=1, keepdims=True)
        grad_scores = (softmax_f * (grad_probs - delta)).astype(jnp.bfloat16)
        grad_query = jnp.dot(grad_scores, key_head, preferred_element_type=jnp.float32) * 0.125
        grad_key = grad_key + contract_rows(grad_scores, query_block) * 0.125
        return ((grad_key, grad_value), grad_query)

    zeros = jnp.zeros(key_head.shape, jnp.float32)
    (grad_key, grad_value), grad_query = lax.scan(
        one_block, (zeros, zeros), (query_head, grad_head, lse_head, allowed_blocks)
    )
    return (grad_query, grad_key, grad_value)


def per_device(
    tokens,
    cotangent,
    clip_frames,
    levels,
    pad_mask,
    w_mod,
    b_mod,
    w_qkv,
    b_qkv,
    w_out,
    b_out,
    w_up,
    b_up,
    w_down,
    b_down,
    noise_table,
):
    gathered = (
        lax.all_gather(w_mod, ("dp", "fsdp"), axis=0, tiled=True),
        lax.all_gather(b_mod, ("dp", "fsdp"), axis=0, tiled=True),
        lax.all_gather(w_qkv, ("dp", "fsdp"), axis=0, tiled=True),
        lax.all_gather(b_qkv, ("dp", "fsdp"), axis=0, tiled=True),
        lax.all_gather(w_out, ("dp", "fsdp"), axis=0, tiled=True),
        lax.all_gather(b_out, ("dp", "fsdp"), axis=0, tiled=True),
        lax.all_gather(w_up, ("dp", "fsdp"), axis=0, tiled=True),
        lax.all_gather(b_up, ("dp", "fsdp"), axis=0, tiled=True),
        lax.all_gather(w_down, ("dp", "fsdp"), axis=0, tiled=True),
        lax.all_gather(b_down, ("dp", "fsdp"), axis=0, tiled=True),
        lax.all_gather(noise_table, ("dp", "fsdp"), axis=0, tiled=True),
    )
    (
        full_wmod,
        full_bmod,
        full_wqkv,
        full_bqkv,
        full_wout,
        full_bout,
        full_wup,
        full_bup,
        full_wdown,
        full_bdown,
        full_table,
    ) = gathered
    tok_count = tokens.shape[0]
    model_width = tokens.shape[1]
    frame_count = levels.shape[0]
    patch_size = tok_count // frame_count
    head_count = model_width // HD
    level_count = full_table.shape[1]
    block_rows = min(tok_count, 512)
    block_count = tok_count // block_rows
    clip_tok, frame_tok = clip_positions(clip_frames[0], patch_size)
    patch_tok = jnp.arange(tok_count, dtype=jnp.int32) % patch_size
    allowed = (
        (clip_tok[:, None] == clip_tok[None, :])
        & (frame_tok[None, :] <= frame_tok[:, None])
        & (pad_mask[None, :] == 1)
    ).reshape(block_count, block_rows, tok_count)
    level_hot = levels[:, None] == jnp.arange(level_count, dtype=jnp.int32)[None, :]
    embedded = jnp.einsum(
        "fl,dl->fd", level_hot.astype(jnp.bfloat16), full_table, preferred_element_type=jnp.float32
    )
    cond_low = jax.nn.silu(embedded).astype(jnp.bfloat16)
    modulation = jnp.dot(
        cond_low, full_wmod, preferred_element_type=jnp.float32
    ) + full_bmod.astype(jnp.float32)
    shift_one, scale_one, gate_one, shift_two, scale_two, gate_two = jnp.split(
        modulation, 6, axis=1
    )
    inputs = tokens.astype(jnp.float32)
    normed_one, inverse_one = normalize(inputs)
    act_one = modulate(normed_one, scale_one, shift_one, frame_count).astype(jnp.bfloat16)
    projected = jnp.dot(act_one, full_wqkv, preferred_element_type=jnp.float32) + full_bqkv.astype(
        jnp.float32
    )
    head_shape = (tok_count, head_count, HD)
    query = rotate(
        projected[:, :model_width].reshape(head_shape), frame_tok, patch_tok, 1.0
    ).astype(jnp.bfloat16)
    keys_rot = rotate(
        projected[:, model_width : 2 * model_width].reshape(head_shape), frame_tok, patch_tok, 1.0
    ).astype(jnp.bfloat16)
    values_low = projected[:, 2 * model_width :].reshape(head_shape).astype(jnp.bfloat16)
    query_heads = jnp.transpose(query, (1, 0, 2)).reshape(head_count, block_count, block_rows, HD)
    key_heads = jnp.transpose(keys_rot, (1, 0, 2))
    value_heads = jnp.transpose(values_low, (1, 0, 2))

    def forward_head(head_items):
        return head_forward(head_items[0], head_items[1], head_items[2], allowed)

    attended_heads, lse_heads = lax.map(forward_head, (query_heads, key_heads, value_heads))
    attended = jnp.transpose(attended_heads.reshape(head_count, tok_count, HD), (1, 0, 2)).reshape(
        tok_count, model_width
    )
    attn_out = jnp.dot(attended, full_wout, preferred_element_type=jnp.float32) + full_bout.astype(
        jnp.float32
    )
    middle = inputs + scale_by(attn_out, gate_one, frame_count)
    normed_two, inverse_two = normalize(middle)
    act_two = modulate(normed_two, scale_two, shift_two, frame_count).astype(jnp.bfloat16)
    hidden_up = jnp.dot(act_two, full_wup, preferred_element_type=jnp.float32) + full_bup.astype(
        jnp.float32
    )
    activated = jax.nn.gelu(hidden_up, approximate=False).astype(jnp.bfloat16)
    branch = jnp.dot(activated, full_wdown, preferred_element_type=jnp.float32) + full_bdown.astype(
        jnp.float32
    )
    block_out = (middle + scale_by(branch, gate_two, frame_count)).astype(jnp.bfloat16)
    back_wmod, back_wqkv, back_wout, back_wup, back_wdown = (
        lax.all_gather(w_mod, ("dp", "fsdp"), axis=0, tiled=True),
        lax.all_gather(w_qkv, ("dp", "fsdp"), axis=0, tiled=True),
        lax.all_gather(w_out, ("dp", "fsdp"), axis=0, tiled=True),
        lax.all_gather(w_up, ("dp", "fsdp"), axis=0, tiled=True),
        lax.all_gather(w_down, ("dp", "fsdp"), axis=0, tiled=True),
    )
    upstream = cotangent.astype(jnp.float32)
    d_gate_two = frame_sum(upstream * branch, frame_count)
    d_branch = scale_by(upstream, gate_two, frame_count).astype(jnp.bfloat16)
    wdown_grad = contract_rows(activated, d_branch)
    bdown_grad = jnp.sum(d_branch, axis=0, dtype=jnp.float32)
    d_hidden = (contract_cols(d_branch, back_wdown) * gelu_slope(hidden_up)).astype(jnp.bfloat16)
    wup_grad = contract_rows(act_two, d_hidden)
    bup_grad = jnp.sum(d_hidden, axis=0, dtype=jnp.float32)
    d_act_two = contract_cols(d_hidden, back_wup)
    d_scale_two = frame_sum(d_act_two * normed_two, frame_count)
    d_shift_two = frame_sum(d_act_two, frame_count)
    d_middle = upstream + normalize_back(
        scale_by(d_act_two, 1.0 + scale_two, frame_count), normed_two, inverse_two
    )
    d_gate_one = frame_sum(d_middle * attn_out, frame_count)
    d_attn = scale_by(d_middle, gate_one, frame_count).astype(jnp.bfloat16)
    wout_grad = contract_rows(attended, d_attn)
    bout_grad = jnp.sum(d_attn, axis=0, dtype=jnp.float32)
    d_attended = contract_cols(d_attn, back_wout).astype(jnp.bfloat16)
    grad_heads = jnp.transpose(d_attended.reshape(head_shape), (1, 0, 2)).reshape(
        head_count, block_count, block_rows, HD
    )

    def backward_head(head_items):
        return head_backward(
            head_items[0], head_items[1], head_items[2], head_items[3], head_items[4], allowed
        )

    d_query_h, d_key_h, d_value_h = lax.map(
        backward_head, (query_heads, key_heads, value_heads, grad_heads, lse_heads)
    )
    d_query = rotate(
        jnp.transpose(d_query_h.reshape(head_count, tok_count, HD), (1, 0, 2)),
        frame_tok,
        patch_tok,
        -1.0,
    )
    d_key = rotate(jnp.transpose(d_key_h, (1, 0, 2)), frame_tok, patch_tok, -1.0)
    d_value = jnp.transpose(d_value_h, (1, 0, 2))
    d_projected = jnp.concatenate(
        [
            d_query.reshape(tok_count, model_width),
            d_key.reshape(tok_count, model_width),
            d_value.reshape(tok_count, model_width),
        ],
        axis=1,
    ).astype(jnp.bfloat16)
    wqkv_grad = contract_rows(act_one, d_projected)
    bqkv_grad = jnp.sum(d_projected, axis=0, dtype=jnp.float32)
    d_act_one = contract_cols(d_projected, back_wqkv)
    d_scale_one = frame_sum(d_act_one * normed_one, frame_count)
    d_shift_one = frame_sum(d_act_one, frame_count)
    token_grad = (
        d_middle
        + normalize_back(scale_by(d_act_one, 1.0 + scale_one, frame_count), normed_one, inverse_one)
    ).astype(jnp.bfloat16)
    d_modulation = jnp.concatenate(
        [d_shift_one, d_scale_one, d_gate_one, d_shift_two, d_scale_two, d_gate_two], axis=1
    ).astype(jnp.bfloat16)
    wmod_grad = contract_rows(cond_low, d_modulation)
    bmod_grad = jnp.sum(d_modulation, axis=0, dtype=jnp.float32)
    sigmoid_e = jax.nn.sigmoid(embedded)
    d_embed = (
        contract_cols(d_modulation, back_wmod) * sigmoid_e * (1.0 + embedded * (1.0 - sigmoid_e))
    )
    summed = (
        lax.psum_scatter(wmod_grad, ("dp", "fsdp"), scatter_dimension=0, tiled=True),
        lax.psum_scatter(bmod_grad, ("dp", "fsdp"), scatter_dimension=0, tiled=True),
        lax.psum_scatter(wqkv_grad, ("dp", "fsdp"), scatter_dimension=0, tiled=True),
        lax.psum_scatter(bqkv_grad, ("dp", "fsdp"), scatter_dimension=0, tiled=True),
        lax.psum_scatter(wout_grad, ("dp", "fsdp"), scatter_dimension=0, tiled=True),
        lax.psum_scatter(bout_grad, ("dp", "fsdp"), scatter_dimension=0, tiled=True),
        lax.psum_scatter(wup_grad, ("dp", "fsdp"), scatter_dimension=0, tiled=True),
        lax.psum_scatter(bup_grad, ("dp", "fsdp"), scatter_dimension=0, tiled=True),
        lax.psum_scatter(wdown_grad, ("dp", "fsdp"), scatter_dimension=0, tiled=True),
        lax.psum_scatter(bdown_grad, ("dp", "fsdp"), scatter_dimension=0, tiled=True),
    )
    table_term = lax.dot_general(
        d_embed,
        level_hot.astype(jnp.float32),
        (((0,), (0,)), ((), ())),
        precision=highest,
        preferred_element_type=jnp.float32,
    )
    table_grad = lax.psum_scatter(table_term, ("dp", "fsdp"), scatter_dimension=0, tiled=True)
    return (
        block_out,
        token_grad,
        summed[0],
        summed[1],
        summed[2],
        summed[3],
        summed[4],
        summed[5],
        summed[6],
        summed[7],
        summed[8],
        summed[9],
        table_grad,
    )


def solution(mesh):
    return jax.shard_map(
        per_device,
        mesh=mesh,
        in_specs=(
            P(("dp", "fsdp"), None),
            P(("dp", "fsdp"), None),
            P(("dp", "fsdp"), None),
            P(("dp", "fsdp")),
            P(("dp", "fsdp")),
            P(("dp", "fsdp"), None),
            P(("dp", "fsdp")),
            P(("dp", "fsdp"), None),
            P(("dp", "fsdp")),
            P(("dp", "fsdp"), None),
            P(("dp", "fsdp")),
            P(("dp", "fsdp"), None),
            P(("dp", "fsdp")),
            P(("dp", "fsdp"), None),
            P(("dp", "fsdp")),
            P(("dp", "fsdp"), None),
        ),
        out_specs=(
            P(("dp", "fsdp"), None),
            P(("dp", "fsdp"), None),
            P(("dp", "fsdp"), None),
            P(("dp", "fsdp")),
            P(("dp", "fsdp"), None),
            P(("dp", "fsdp")),
            P(("dp", "fsdp"), None),
            P(("dp", "fsdp")),
            P(("dp", "fsdp"), None),
            P(("dp", "fsdp")),
            P(("dp", "fsdp"), None),
            P(("dp", "fsdp")),
            P(("dp", "fsdp"), None),
        ),
        check_vma=False,
    )
```

profile of v0, /device:TPU:0, one launch (start us, length us, event | category | flops | bytes accessed | tf_op | source)
XLA Modules:
  0.0 2304.7 jit_solution(8416402026612398978)
XLA Ops:
  16.7 42.5 %all-reduce.10 = (bf16[3072]{0:T(1024)(128)(2,1)S(1)}, bf16[6144]{0:T(1024)(128)(2,1)S(1)}, bf16[1024]{0:T(1024)(128)(2,1)S(1)}, bf16[1024]{0:T(1024)(128)(2,1)S(1)}) all-reduce(bf16[3072]{0:T(1024)(128)(2,1)S(1)} %dynamic-update-slice.1, bf16[6144]{0:T(1024)(128)(2,1)S(1)} %dynamic-update-slice, ...), channel_id=1, replica_groups=mesh['dp'=4,'fsdp'=8] {'dp','fsdp'}, use_global_device_ids=true, to_apply=%add.1 | all-reduce | flops 11264 | bytes 45056
  65.1 40.2 %all-gather = bf16[32,1,128]{2,1,0:T(2,128)(2,1)S(1)} all-gather(bf16[1,1,128]{2,1,0:T(2,128)(2,1)S(1)} %bitcast.285), channel_id=1, replica_groups=mesh['dp'=4,'fsdp'=8] {'dp','fsdp'}, dimensions={0}, use_global_device_ids=true | all-gather | bytes 8448 | tf_op jit(solution)/shard_map/all_gather | solution.py:161
  110.0 57.5 %all-gather.10.cloned.1.call-done = bf16[1024,6144]{1,0:T(8,128)(2,1)} async-done(((bf16[32,6144]{1,0:T(8,128)(2,1)}), bf16[1024,6144]{1,0:T(8,128)(2,1)}) %all-gather.10.cloned.1.call-update) | async-done | bytes 12582928 | tf_op jit(solution)/shard_map/all_gather | solution.py:154
  167.5 6.3 convolution_add_fusion.1
  176.9 61.5 %all-gather.12.cloned.1.call-done = bf16[1024,3072]{1,0:T(8,128)(2,1)} async-done(((bf16[32,3072]{1,0:T(8,128)(2,1)}), bf16[1024,3072]{1,0:T(8,128)(2,1)}) %all-gather.12.cloned.1.call-update) | async-done | bytes 6291472 | tf_op jit(solution)/shard_map/all_gather | solution.py:156
  238.5 9.6 broadcast_add_fusion
  253.8 5.4 copy.65
  259.1 5.3 copy.64
  264.5 4.9 subtract_convert_fusion.2
  285.3 273.0 %while.58 = (s32[]{:T(128)}, bf16[16,2,512,64]{2,1,3,0:T(2,128)(2,1)}, f32[16,2,512]{2,1,0:T(2,128)}, bf16[16,2,512,64]{3,2,1,0:T(8,128)(2,1)}, bf16[16,1024,64]...) while((s32[]{:T(128)}, ...), condition=%wide.region_10.11_spmd.clone, body=%wide.region_5.10_spmd.clone.sunk | while | flops 142638592 | bytes 9551178 | solution.py:226
  290.6 9.7 while.61
  307.7 9.7 while.61
  324.7 9.7 while.61
  341.8 9.8 while.61
  358.9 9.7 while.61
  376.0 9.7 while.61
  393.0 9.7 while.61
  410.1 9.7 while.61
  427.2 9.7 while.61
  444.2 9.7 while.61
  461.3 9.7 while.61
  478.4 9.7 while.61
  495.4 9.7 while.61
  512.5 9.7 while.61
  529.5 9.7 while.61
  546.6 9.7 while.61
  567.4 7.0 fusion.82
  578.7 48.1 %fusion.29 = (bf16[1024,4096]{1,0:T(8,128)(2,1)}, f32[1024,4096]{1,0:T(8,128)}) fusion(f32[4096]{0:T(1024)S(1)} %bitcast.283, bf16[1024,1024]{1,0:T(8,128)(2,1)} %fusion.58, bf16[1024,4096]{1,0:T(8,128)(2,1)} %all-gather.16.cloned.1.call-done), kind=kOutput, calls=%fused_computation.56 | convolution fusion | flops 8866758656 | bytes 35667968 | tf_op jit(solution)/shard_map/dot_general | solution.py:236
  626.9 20.0 convert_reduce_fusion
  646.8 14.3 fusion.63
  662.9 18.5 convert_reduce_fusion.4
  689.2 493.6 %while.60 = (s32[]{:T(128)}, f32[16,2,512,64]{2,1,3,0:T(2,128)}, f32[16,1024,64]{1,2,0:T(8,128)}, bf16[16,1024,64]{1,2,0:T(8,128)(2,1)}, bf16[16,2,512,64]{3,2,1...) while((s32[]{:T(128)}, f32[16,2,512,64]{2,1,3,0:T(2,128)}, ...), condition=%wide.region_19.20_spmd.clone, body=%wide.region_15.19_spmd.clone.sunk | while | flops 344817152 | bytes 22191524 | solution.py:279
  698.5 17.9 while.62
  729.3 17.9 while.62
  760.2 17.9 while.62
  791.0 17.9 while.62
  821.9 17.9 while.62
  852.7 17.9 while.62
  883.5 17.9 while.62
  914.4 17.9 while.62
  945.2 17.9 while.62
  976.1 17.9 while.62
  1007.0 17.9 while.62
  1037.8 17.9 while.62
  1068.7 17.9 while.62
  1099.5 17.9 while.62
  1130.3 17.9 while.62
  1161.2 17.9 while.62
  1182.8 6.9 reshape.337
  1189.7 4.9 subtract_convert_fusion.1
  1197.1 12.9 fusion.62
  1227.3 6.5 fusion.86
  1234.4 14.7 fusion.78
  1249.2 16.2 fusion.87
  1265.6 10.2 fusion.77
  1275.9 16.2 fusion.88
  1296.6 40.8 %all-reduce.9 = (f32[6144]{0:T(1024)S(1)}, f32[3072]{0:T(1024)S(1)}, f32[1024]{0:T(1024)S(1)}, f32[4096]{0:T(1024)S(1)}, f32[1024]{0:T(1024)S(1)}) all-reduce(f32[6144]{0:T(1024)S(1)} %convert_reduce_fusion.5, f32[3072]{0:T(1024)S(1)} %convert_reduce_fusion.1, ...), channel_id=3, replica_groups=mesh['dp'=4,'fsdp'=8] {'dp','fsdp'}, use_global_device_ids=true, to_apply=%region_30.31.clone | all-reduce | flops 15360 | bytes 122880
  1340.4 5.2 fusion.52
  1345.6 24.4 %reduce-scatter.17.cloned.1.call-done = f32[32,1000]{1,0:T(8,128)} async-done(((f32[1024,1000]{1,0:T(8,128)}), f32[32,1000]{1,0:T(8,128)}) %reduce-scatter.17.cloned.1.call-update) | async-done | bytes 128016 | tf_op jit(solution)/shard_map/reduce_scatter | solution.py:335
  1370.0 144.8 %reduce-scatter.11.cloned.1.call-done = f32[32,1024]{1,0:T(8,128)} async-done(((f32[1024,1024]{1,0:T(8,128)}), f32[32,1024]{1,0:T(8,128)}) %reduce-scatter.11.cloned.1.call-update) | async-done | bytes 131088 | tf_op jit(solution)/shard_map/reduce_scatter | solution.py:321
  1514.8 158.1 %reduce-scatter.9.cloned.1.call-done = f32[32,3072]{1,0:T(8,128)} async-done(((f32[1024,3072]{1,0:T(8,128)}), f32[32,3072]{1,0:T(8,128)}) %reduce-scatter.9.cloned.1.call-update) | async-done | bytes 393232 | tf_op jit(solution)/shard_map/reduce_scatter | solution.py:319
  1672.9 188.2 %reduce-scatter.13.cloned.1.call-done = f32[32,4096]{1,0:T(8,128)} async-done(((f32[1024,4096]{1,0:T(8,128)}), f32[32,4096]{1,0:T(8,128)}) %reduce-scatter.13.cloned.1.call-update) | async-done | bytes 524304 | tf_op jit(solution)/shard_map/reduce_scatter | solution.py:323
  1861.0 247.9 %reduce-scatter.7.cloned.1.call-done = f32[32,6144]{1,0:T(8,128)} async-done(((f32[1024,6144]{1,0:T(8,128)}), f32[32,6144]{1,0:T(8,128)}) %reduce-scatter.7.cloned.1.call-update) | async-done | bytes 786448 | tf_op jit(solution)/shard_map/reduce_scatter | solution.py:317
  2108.9 188.8 %reduce-scatter.15.cloned.1.call-done = f32[128,1024]{1,0:T(8,128)} async-done(((f32[4096,1024]{1,0:T(8,128)}), f32[128,1024]{1,0:T(8,128)}) %reduce-scatter.15.cloned.1.call-update) | async-done | bytes 524304 | tf_op jit(solution)/shard_map/reduce_scatter | solution.py:325
  (890 shorter events, 860.1 us)
Async XLA Ops:
  7.2 54.0 %copy-start.2 = (bf16[1024,1024]{1,0:T(8,128)(2,1)S(1)}, bf16[1024,1024]{1,0:T(8,128)(2,1)}, u32[]{:S(2)}) copy-start(bf16[1024,1024]{1,0:T(8,128)(2,1)} %param.24) | copy-start | bytes 6291460
  7.2 56.8 %copy-start.44 = (s32[1024]{0:T(1024)S(1)}, s32[1024]{0:T(1024)}, u32[]{:S(2)}) copy-start(s32[1024]{0:T(1024)} %param.28) | copy-start | bytes 12292
  7.2 57.9 %copy-start.47 = (bf16[128]{0:T(256)(128)(2,1)S(1)}, bf16[128]{0:T(256)(128)(2,1)}, u32[]{:S(2)}) copy-start(bf16[128]{0:T(256)(128)(2,1)} %param.36) | copy-start | bytes 772
  7.2 100.5 %copy-start.45 = (s32[4]{0:T(128)S(1)}, s32[4]{0:T(128)}, u32[]{:S(2)}) copy-start(s32[4]{0:T(128)} %param.27) | copy-start | bytes 52
  7.2 100.5 %all-gather.8.cloned.1.call-start = ((), (), s32[]{:S(2)}) async-start(), calls=%async_computation.6 | async-start | bytes 2162688 | tf_op jit(solution)/shard_map/all_gather | solution.py:164
  8.0 159.6 %all-gather.10.cloned.1.call-start = ((), (), s32[]{:S(2)}) async-start(), calls=%async_computation.7 | async-start | bytes 12976128 | tf_op jit(solution)/shard_map/all_gather | solution.py:154
  8.7 229.8 %all-gather.12.cloned.1.call-start = ((), (), s32[]{:S(2)}) async-start(), calls=%async_computation.8 | async-start | bytes 6488064 | tf_op jit(solution)/shard_map/all_gather | solution.py:156
  9.4 557.9 %all-gather.14.cloned.1.call-start = ((), (), s32[]{:S(2)}) async-start(), calls=%async_computation.9 | async-start | bytes 2162688 | tf_op jit(solution)/shard_map/all_gather | solution.py:158
  10.0 568.7 %all-gather.16.cloned.1.call-start = ((), (), s32[]{:S(2)}) async-start(), calls=%async_computation.10 | async-start | bytes 8650752 | tf_op jit(solution)/shard_map/all_gather | solution.py:160
  10.6 616.2 %all-gather.18.cloned.1.call-start = ((), (), s32[]{:S(2)}) async-start(), calls=%async_computation.11 | async-start | bytes 8650752 | tf_op jit(solution)/shard_map/all_gather | solution.py:162
  11.2 1358.9 %reduce-scatter.17.cloned.1.call-start = ((), (), s32[]{:S(2)}) async-start(), calls=%async_computation.17 | async-start | bytes 4325376 | tf_op jit(solution)/shard_map/reduce_scatter | solution.py:335
  61.2 113.3 %copy-start.25 = (f32[1024]{0:T(1024)}, f32[1024]{0:T(1024)S(1)}, u32[]{:S(2)}) copy-start(f32[1024]{0:T(1024)S(1)} %broadcast_multiply_fusion.8) | copy-start | bytes 12292
  61.9 112.6 %copy-start.30 = (f32[1024]{0:T(1024)}, f32[1024]{0:T(1024)S(1)}, u32[]{:S(2)}) copy-start(f32[1024]{0:T(1024)S(1)} %add_rsqrt_fusion.1) | copy-start | bytes 12292
  107.7 156.7 %copy-start.10 = (f32[1024,32]{0,1:T(8,128)}, f32[1024,32]{0,1:T(8,128)S(1)}, u32[]{:S(2)}) copy-start(f32[1024,32]{0,1:T(8,128)S(1)} %get-tuple-element.547) | copy-start | bytes 393220
  110.0 63.8 %copy-start.15 = (f32[4,1024]{1,0:T(4,128)}, f32[4,1024]{1,0:T(4,128)S(1)}, u32[]{:S(2)}) copy-start(f32[4,1024]{1,0:T(4,128)S(1)} %fusion.69) | copy-start | bytes 49156
  174.5 73.6 %copy-start.17 = (f32[4,1024]{1,0:T(4,128)}, f32[4,1024]{1,0:T(4,128)S(1)}, u32[]{:S(2)}) copy-start(f32[4,1024]{1,0:T(4,128)S(1)} %get-tuple-element.553) | copy-start | bytes 49156
  558.3 9.0 copy-start.12
  558.3 4.8 copy-start.19
  558.3 9.0 copy-start.3
  558.4 9.0 copy-start.23
  558.4 9.0 copy-start.34
  574.4 2.0 copy-start
  574.4 2.0 copy-start.21
  574.4 2.0 copy-start.29
  574.4 2.0 copy-start.27
  574.9 3.8 copy-start.41
  575.0 1.4 copy-start.32
  578.7 48.1 %copy-start.9 = (bf16[1024,1024]{1,0:T(8,128)(2,1)S(1)}, bf16[1024,1024]{1,0:T(8,128)(2,1)}, u32[]{:S(2)}) copy-start(bf16[1024,1024]{1,0:T(8,128)(2,1)} %get-tuple-element.516) | copy-start | bytes 6291460
  626.8 20.0 copy-start.1
  626.8 20.0 copy-start.22
  626.8 20.0 copy-start.28
  626.9 20.0 copy-start.33
  661.2 1.7 copy-start.6
  661.2 1.7 copy-start.20
  661.2 1.7 copy-start.24
  661.2 1.7 copy-start.36
  686.0 3.2 copy-start.13
  1182.8 6.9 copy-start.11
  1182.8 6.9 copy-start.14
  1194.6 2.5 copy-start.4
  1194.6 2.5 copy-start.18
  1194.6 2.5 copy-start.26
  1194.6 2.5 copy-start.31
  1194.8 2.0 copy-start.8
  1197.1 22.9 slice-start
  1197.1 22.9 slice-start.1
  1210.0 3.2 copy-start.7
  1210.0 3.2 copy-start.37
  1210.0 10.1 slice-start.2
  1213.2 3.5 copy-start.5
  1213.2 3.4 copy-start.35
  1216.6 3.3 copy-start.39
  1216.6 3.3 copy-start.38
  1216.6 3.4 copy-start.16
  1220.1 3.4 copy-start.46
  1227.3 287.5 %reduce-scatter.11.cloned.1.call-start = ((), (), s32[]{:S(2)}) async-start(), calls=%async_computation.14 | async-start | bytes 4325376 | tf_op jit(solution)/shard_map/reduce_scatter | solution.py:321
  1233.9 439.0 %reduce-scatter.9.cloned.1.call-start = ((), (), s32[]{:S(2)}) async-start(), calls=%async_computation.13 | async-start | bytes 12976128 | tf_op jit(solution)/shard_map/reduce_scatter | solution.py:319
  1249.1 611.9 %reduce-scatter.13.cloned.1.call-start = ((), (), s32[]{:S(2)}) async-start(), calls=%async_computation.15 | async-start | bytes 17301504 | tf_op jit(solution)/shard_map/reduce_scatter | solution.py:323
  1265.4 843.5 %reduce-scatter.7.cloned.1.call-start = ((), (), s32[]{:S(2)}) async-start(), calls=%async_computation.12 | async-start | bytes 25952256 | tf_op jit(solution)/shard_map/reduce_scatter | solution.py:317
  1275.8 1021.9 %reduce-scatter.15.cloned.1.call-start = ((), (), s32[]{:S(2)}) async-start(), calls=%async_computation.16 | async-start | bytes 17301504 | tf_op jit(solution)/shard_map/reduce_scatter | solution.py:325
  1292.1 4.5 copy-start.40
  1292.1 4.5 copy-start.42
  1292.1 4.5 copy-start.43
Sparse Core Ops, SparseCore 0:
  11.0 59.1 all-gather.7
  73.2 94.2 all-gather.9
  170.6 67.8 all-gather.11
  241.3 54.8 all-gather.13
  299.1 76.0 all-gather.15
  378.0 75.8 all-gather.17
  1227.4 142.5 reduce-scatter.16
  1372.9 141.8 reduce-scatter.10
  1521.4 151.4 reduce-scatter.8
  1675.6 185.4 reduce-scatter.12
  1868.1 240.8 reduce-scatter.6
  2111.6 186.0 reduce-scatter.14
where the time goes:
time: 2320 us; the launch traced here: 2300 us
  waiting for transfers between devices  1070 us (46%)
  matrix products  588 us (25%)
  local copies, waits for them, and re-layouts  353 us (15%)
  other arithmetic  148 us (6%)
  blocking collectives  124 us (5%)
    reduce_scatter x1, waiting for transfers between devices, per_device(): lax.psum_scatter(wmod_grad, ('dp', 'fsdp'), scatter_dimension=0, tiled=True)  248 us
    dot_general x101, matrix products, contract_cols(): lax.dot_general(left, right, (((1,), (1,)), ((), ())), preferred_element_...  215 us
    dot_general x69, matrix products, contract_rows(): lax.dot_general(left, right, (((0,), (0,)), ((), ())), preferred_element_...  192 us
    reduce_scatter x1, waiting for transfers between devices, per_device(): lax.psum_scatter(wdown_grad, ('dp', 'fsdp'), scatter_dimension=0, tiled=T...  189 us
    reduce_scatter x1, waiting for transfers between devices, per_device(): lax.psum_scatter(wup_grad, ('dp', 'fsdp'), scatter_dimension=0, tiled=True)  188 us
    reduce_scatter x1, waiting for transfers between devices, per_device(): lax.psum_scatter(wqkv_grad, ('dp', 'fsdp'), scatter_dimension=0, tiled=True)  158 us
    squeeze x96, local copies, waits for them, and re-layouts, per_device(): lax.map(forward_head, (query_heads, key_heads, value_heads))  151 us
    reduce_scatter x1, waiting for transfers between devices, per_device(): lax.psum_scatter(wout_grad, ('dp', 'fsdp'), scatter_dimension=0, tiled=True)  145 us
  transfers between devices with their start and end apart: 12, of which 8 were waited for; matrix products, arithmetic and copies ran while one was open for 21% of the time, Pallas kernels for 0%

commit v1 on v0

v1 whole, which is shorter than its diff:
```python
import jax
import jax.numpy as jnp
from jax import lax
from jax.experimental import pallas as pl
from jax.experimental.pallas import tpu as pltpu
from jax.sharding import PartitionSpec as P

bf16 = jnp.bfloat16
f32 = jnp.float32
AXES = ("dp", "fsdp")
HD = 64
LANE = 128
EPS = 1e-06
NN = (((1,), (0,)), ((), ()))
NT = (((1,), (1,)), ((), ()))
TN = (((0,), (0,)), ((), ()))


def dot(left, right, dims):
    return lax.dot_general(left, right, dims, preferred_element_type=f32)


def lanes(shape):
    return lax.broadcasted_iota(jnp.int32, shape, 1)


def normalize(values):
    centred = values - jnp.mean(values, axis=1, keepdims=True)
    inverse = lax.rsqrt(jnp.mean(centred * centred, axis=1, keepdims=True) + EPS)
    return centred * inverse, inverse


def normalize_back(grad, normed, inverse):
    return inverse * (
        grad
        - jnp.mean(grad, axis=1, keepdims=True)
        - normed * jnp.mean(grad * normed, axis=1, keepdims=True)
    )


def col_sum(values):
    return jnp.sum(values.astype(f32), axis=0, keepdims=True)


def partner(values):
    return jnp.where(
        lanes(values.shape) % HD < HD // 2,
        pltpu.roll(values, LANE - HD // 2, 1),
        pltpu.roll(values, HD // 2, 1),
    )


def carry_lanes(values):
    sub = lanes(values.shape) % HD
    high = values.astype(bf16).astype(f32)
    rest = values - high
    mid = rest.astype(bf16).astype(f32)
    return jnp.where(
        sub == 8, high, jnp.where(sub == 9, mid, jnp.where(sub == 10, rest - mid, 0.0))
    )


def qkv_kernel(x_ref, mod_ref, w_ref, b_ref, cos_ref, sin_ref, act_ref, q_ref, k_ref, v_ref):
    normed, _ = normalize(x_ref[...].astype(f32))
    act = (normed * (1.0 + mod_ref[0, 1:2, :]) + mod_ref[0, 0:1, :]).astype(bf16)
    act_ref[...] = act
    width = x_ref.shape[1]
    cosine, sine = cos_ref[...], sin_ref[...]
    step = 2 * LANE
    for col in range(0, 3 * width, step):
        raw = dot(act, w_ref[:, col : col + step], NN) + b_ref[:, col : col + step].astype(f32)
        for sub in range(0, step, LANE):
            part = raw[:, sub : sub + LANE]
            at = (col + sub) % width
            if col < width:
                part = (part * cosine + partner(part) * sine).astype(bf16)
                q_ref[:, at : at + LANE] = (part.astype(f32) * 0.125).astype(bf16)
            elif col < 2 * width:
                k_ref[:, at : at + LANE] = (part * cosine + partner(part) * sine).astype(bf16)
            else:
                v_ref[:, at : at + LANE] = part.astype(bf16)


def attention_forward(q_ref, k_ref, v_ref, see_ref, hot_ref, out_ref, aug_ref, *, frames):
    rows_all = q_ref.shape[0]
    size = rows_all // frames
    low = lanes((rows_all, LANE)) < HD
    low_b = lanes((size, LANE)) < HD
    k, v, see = k_ref[...], v_ref[...], see_ref[...]
    one = jnp.ones_like(v)
    keys = (jnp.where(low, k, see), jnp.where(low, see, k))
    vals = (jnp.where(low, v, one), jnp.where(low, one, v))
    for i in range(frames):
        rows = slice(i * size, (i + 1) * size)
        width = (i + 1) * size
        q, hot = q_ref[rows, :], hot_ref[rows, :]
        query = (jnp.where(low_b, q, hot), jnp.where(low_b, hot, q))
        tops, outs = [], []
        for h in range(2):
            scores = dot(query[h], keys[h][:width], NT)
            top = jnp.max(scores, axis=1, keepdims=True)
            expo = jnp.exp(scores - top).astype(bf16)
            outs.append(dot(expo, vals[h][:width], NN))
            tops.append(top)
        num = jnp.where(low_b, outs[0], outs[1])
        den = jnp.where(low_b, outs[1], outs[0])
        out_ref[rows, :] = (num / pltpu.roll(den, HD, 1)).astype(bf16)
        lse = jnp.where(low_b, tops[1], tops[0]) + jnp.log(den)
        aug_ref[rows, :] = (carry_lanes(-lse) + hot.astype(f32)).astype(bf16)


def project_kernel(att_ref, x_ref, mod_ref, w_ref, b_ref, middle_ref, attn_ref, act_ref):
    attn = dot(att_ref[...], w_ref[...], NN) + b_ref[...].astype(f32)
    attn_ref[...] = attn.astype(bf16)
    middle = x_ref[...].astype(f32) + mod_ref[0, 2:3, :] * attn
    middle_ref[...] = middle
    normed, _ = normalize(middle)
    act_ref[...] = (normed * (1.0 + mod_ref[0, 4:5, :]) + mod_ref[0, 3:4, :]).astype(bf16)


def up_kernel(act_ref, w_ref, b_ref, out_ref, slope_ref):
    hidden = dot(act_ref[...], w_ref[...], NN) + b_ref[...].astype(f32)
    share = 0.5 * (1.0 + lax.erf(hidden * 0.7071067811865476))
    out_ref[...] = (hidden * share).astype(bf16)
    slope = share + hidden * jnp.exp(-0.5 * hidden * hidden) * 0.3989422804014327
    slope_ref[...] = slope.astype(bf16)


def down_kernel(
    act_ref, w_ref, b_ref, mid_ref, cot_ref, mod_ref, out_ref, dbr_ref, gate_ref, sum_ref, acc_ref
):
    step, last = pl.program_id(0), pl.num_programs(0) - 1
    part = dot(act_ref[...], w_ref[...], NN)

    @pl.when(step == 0)
    def _():
        acc_ref[...] = part

    @pl.when(step > 0)
    def _():
        acc_ref[...] += part

    @pl.when(step == last)
    def _():
        frames = mod_ref.shape[0]
        size = acc_ref.shape[0] // frames
        total = jnp.zeros((1, acc_ref.shape[1]), f32)
        for i in range(frames):
            rows = slice(i * size, (i + 1) * size)
            gate = mod_ref[i, 5:6, :]
            branch = acc_ref[rows, :] + b_ref[...].astype(f32)
            out_ref[rows, :] = (mid_ref[rows, :] + gate * branch).astype(bf16)
            upstream = cot_ref[rows, :].astype(f32)
            d_branch = (upstream * gate).astype(bf16)
            dbr_ref[rows, :] = d_branch
            gate_ref[i : i + 1, :] = col_sum(upstream * branch)
            total += col_sum(d_branch)
        sum_ref[...] = total


def hidden_back_kernel(dbr_ref, w_ref, slope_ref, out_ref, sum_ref):
    d_hidden = (dot(dbr_ref[...], w_ref[...], NT) * slope_ref[...].astype(f32)).astype(bf16)
    out_ref[...] = d_hidden
    sum_ref[...] = col_sum(d_hidden)


def mlp_back_kernel(
    dh_ref, w_ref, mid_ref, cot_ref, attn_ref, mod_ref, dmid_ref, datt_ref, stat_ref, sum_ref, acc_ref
):
    step, last = pl.program_id(0), pl.num_programs(0) - 1
    part = dot(dh_ref[...], w_ref[...], NT)

    @pl.when(step == 0)
    def _():
        acc_ref[...] = part

    @pl.when(step > 0)
    def _():
        acc_ref[...] += part

    @pl.when(step == last)
    def _():
        frames = mod_ref.shape[0]
        size = acc_ref.shape[0] // frames
        total = jnp.zeros((1, acc_ref.shape[1]), f32)
        for i in range(frames):
            rows = slice(i * size, (i + 1) * size)
            d_act = acc_ref[rows, :]
            normed, inverse = normalize(mid_ref[rows, :])
            stat_ref[i, 1:2, :] = col_sum(d_act)
            stat_ref[i, 2:3, :] = col_sum(d_act * normed)
            d_middle = cot_ref[rows, :].astype(f32) + normalize_back(
                d_act * (1.0 + mod_ref[i, 4:5, :]), normed, inverse
            )
            dmid_ref[rows, :] = d_middle
            stat_ref[i, 0:1, :] = col_sum(d_middle * attn_ref[rows, :].astype(f32))
            d_attn = (d_middle * mod_ref[i, 2:3, :]).astype(bf16)
            datt_ref[rows, :] = d_attn
            total += col_sum(d_attn)
        sum_ref[...] = total


def attention_backward(
    q_ref, k_ref, v_ref, do_ref, o_ref, aug_ref, see_ref, cos_ref, sin_ref, out_ref, sum_ref, acc_ref, *, frames
):
    rows_all = q_ref.shape[0]
    size = rows_all // frames
    low = lanes((rows_all, LANE)) < HD
    q, aug, grad = q_ref[...], aug_ref[...], do_ref[...]
    prod = grad.astype(f32) * o_ref[...].astype(f32)
    delta_low = jnp.sum(jnp.where(low, prod, 0.0), axis=1, keepdims=True)
    delta_high = jnp.sum(jnp.where(low, 0.0, prod), axis=1, keepdims=True)
    grad_aug = carry_lanes(jnp.where(low, -delta_high, -delta_low)).astype(bf16)
    query = (jnp.where(low, q, aug), jnp.where(low, aug, q))
    upper = (jnp.where(low, grad, grad_aug), jnp.where(low, grad_aug, grad))
    low_b = lanes((size, LANE)) < HD
    sub = lanes((size, LANE)) % HD
    ones = jnp.where((sub >= 8) & (sub <= 10), 1.0, 0.0).astype(bf16)
    sum_k = sum_v = jnp.zeros((1, LANE), f32)
    for j in range(frames):
        rows = slice(j * size, (j + 1) * size)
        start = j * size
        k, v, see = k_ref[rows, :], v_ref[rows, :], see_ref[rows, :] + ones
        keys = (jnp.where(low_b, k, see), jnp.where(low_b, see, k))
        vals = (jnp.where(low_b, v, ones), jnp.where(low_b, ones, v))
        dvs, dks, dqs = [], [], []
        for h in range(2):
            probs = jnp.exp(dot(keys[h], query[h][start:], NT))
            d_scores = (probs * dot(vals[h], upper[h][start:], NT)).astype(bf16)
            dvs.append(dot(probs.astype(bf16), grad[start:], NN))
            dks.append(dot(d_scores, q[start:], NN))
            dqs.append(dot(d_scores, k, TN))
        d_value = jnp.where(low_b, dvs[0], dvs[1]).astype(bf16)
        d_key = jnp.where(low_b, dks[0], dks[1])
        d_key = (d_key * cos_ref[rows, :] - partner(d_key) * sin_ref[rows, :]).astype(bf16)
        out_ref[1, rows, :] = d_key
        out_ref[2, rows, :] = d_value
        sum_k = sum_k + col_sum(d_key)
        sum_v = sum_v + col_sum(d_value)
        d_query = jnp.where(lanes(dqs[0].shape) < HD, dqs[0], dqs[1])
        if j == 0:
            acc_ref[...] = d_query
        else:
            acc_ref[start:, :] += d_query
    d_query = acc_ref[...] * 0.125
    d_query = (d_query * cos_ref[...] - partner(d_query) * sin_ref[...]).astype(bf16)
    out_ref[0] = d_query
    sum_ref[0, 0:1, :] = col_sum(d_query)
    sum_ref[0, 1:2, :] = sum_k
    sum_ref[0, 2:3, :] = sum_v


def input_back_kernel(dp_ref, w_ref, x_ref, dmid_ref, mod_ref, out_ref, stat_ref, acc_ref):
    step, last = pl.program_id(0), pl.num_programs(0) - 1
    part = dot(dp_ref[0], w_ref[...], NT)

    @pl.when(step == 0)
    def _():
        acc_ref[...] = part

    @pl.when(step > 0)
    def _():
        acc_ref[...] += part

    @pl.when(step == last)
    def _():
        frames = mod_ref.shape[0]
        size = acc_ref.shape[0] // frames
        for i in range(frames):
            rows = slice(i * size, (i + 1) * size)
            d_act = acc_ref[rows, :]
            normed, inverse = normalize(x_ref[rows, :].astype(f32))
            stat_ref[i, 0:1, :] = col_sum(d_act)
            stat_ref[i, 1:2, :] = col_sum(d_act * normed)
            back = normalize_back(d_act * (1.0 + mod_ref[i, 1:2, :]), normed, inverse)
            out_ref[rows, :] = (dmid_ref[rows, :] + back).astype(bf16)


def weight_grad_kernel(left_ref, right_ref, out_ref):
    out_ref[...] = dot(left_ref[...], right_ref[...], TN).astype(bf16)


def qkv_grad_kernel(left_ref, right_ref, out_ref):
    out_ref[...] = dot(left_ref[...], right_ref[0], TN).astype(bf16)


def like(shape, kind):
    return jax.ShapeDtypeStruct(shape, kind)


def whole(shape):
    return pl.BlockSpec(shape, lambda i: (0,) * len(shape))


def by_rows(size, width):
    return pl.BlockSpec((size, width), lambda i: (i, 0))


def by_cols(height, size):
    return pl.BlockSpec((height, size), lambda i: (0, i))


def run(kernel, grid, ins, outs, shapes, args, scratch=(), name=None, flops=0):
    moved = sum(a.size * a.dtype.itemsize for a in args)
    return pl.pallas_call(
        kernel,
        grid=(grid,),
        in_specs=ins,
        out_specs=outs,
        out_shape=shapes,
        scratch_shapes=list(scratch),
        name=name,
        cost_estimate=pl.CostEstimate(flops=flops, bytes_accessed=2 * moved, transcendentals=0),
        compiler_params=pltpu.CompilerParams(vmem_limit_bytes=60 * 1024 * 1024),
    )(*args)


def tables(clip_row, pad, count):
    frames = clip_row.shape[0]
    size = count // frames
    slots = jnp.arange(frames, dtype=jnp.int32)
    ends = jnp.sum(jnp.where(slots[None, :] <= slots[:, None], clip_row[None, :], 0), axis=1)
    clip_of = jnp.sum((slots[:, None] >= ends[None, :]).astype(jnp.int32), axis=1)
    starts = ends - clip_row
    start_of = jnp.sum(jnp.where(clip_of[:, None] == slots[None, :], starts[None, :], 0), axis=1)
    frame_pos = slots - start_of
    frame = jnp.arange(count, dtype=jnp.int32) // size
    lane = jnp.arange(LANE, dtype=jnp.int32) % HD
    frame_hot = frame[:, None] == lane[None, :]
    own = frame[:, None] == slots[None, :]
    clip_tok = jnp.sum(jnp.where(own, clip_of[None, :], 0), axis=1)
    pos_tok = jnp.sum(jnp.where(own, frame_pos[None, :], 0), axis=1)
    lane_own = lane[:, None] == slots[None, :]
    lane_clip = jnp.sum(jnp.where(lane_own, clip_of[None, :], 0), axis=1)
    lane_pos = jnp.sum(jnp.where(lane_own, frame_pos[None, :], 0), axis=1)
    seen = (
        (clip_tok[:, None] == lane_clip[None, :])
        & (pos_tok[:, None] <= lane_pos[None, :])
        & (pad[:, None] == 1)
    )
    see = jnp.where((lane[None, :] < frames) & ~seen, -1e30, 0.0).astype(bf16)
    quarter = HD // 4
    freq = 10000.0 ** (-jnp.arange(quarter, dtype=f32) / quarter)
    patch = jnp.arange(count, dtype=jnp.int32) % size
    angle = jnp.concatenate(
        [pos_tok.astype(f32)[:, None] * freq[None, :], patch.astype(f32)[:, None] * freq[None, :]],
        axis=1,
    )
    cosine, sine = jnp.cos(angle), jnp.sin(angle)
    cosine = jnp.concatenate([cosine] * 4, axis=1)
    sine = jnp.concatenate([-sine, sine, -sine, sine], axis=1)
    return see, frame_hot.astype(bf16), cosine, sine


def per_device(
    tokens, cotangent, clip_frames, levels, pad_mask, w_mod, b_mod, w_qkv, b_qkv, w_out, b_out,
    w_up, b_up, w_down, b_down, noise_table,
):
    count, width = tokens.shape
    frames = levels.shape[0]
    size = count // frames
    hidden = w_up.shape[1]
    ndev = width // w_up.shape[0]
    me = lax.axis_index("dp") * lax.axis_size("fsdp") + lax.axis_index("fsdp")

    def gather(value):
        return lax.all_gather(value, AXES, axis=0, tiled=True)

    def scatter(value):
        return lax.psum_scatter(value, AXES, scatter_dimension=0, tiled=True)

    all_levels = gather(levels)
    hot = (all_levels[:, None] == jnp.arange(noise_table.shape[1], dtype=jnp.int32)[None, :]).astype(bf16)
    embedded = dot(hot, noise_table, NT)
    cond = jax.nn.silu(embedded).astype(bf16)
    partial = dot(cond, w_mod, NN)
    biases = [b_mod, b_qkv, b_out, b_up, b_down]
    lengths = [b.shape[0] for b in biases]
    packed = jnp.concatenate(biases)
    packed = jnp.pad(packed, (0, -packed.shape[0] % (8 * LANE))).reshape(8, -1)
    packed = gather(packed).reshape(ndev, -1)
    full_bias, at = [], 0
    for length in lengths:
        full_bias.append(packed[:, at : at + length].reshape(1, -1))
        at += length
    bias_mod, bias_qkv, bias_out, bias_up, bias_down = full_bias
    modulation = (scatter(partial) + bias_mod.astype(f32)).reshape(frames, 6, width)
    full_qkv, full_out, full_up, full_down = gather(w_qkv), gather(w_out), gather(w_up), gather(w_down)
    see, frame_hot, cosine, sine = tables(clip_frames[0], pad_mask, count)

    acts = like((count, width), bf16)
    wide = like((count, width), f32)
    tall = like((count, hidden), bf16)
    row = whole((1, width))
    mod_row = pl.BlockSpec((1, 6, width), lambda i: (i, 0, 0))
    mod_all = whole((frames, 6, width))
    rows_bf = by_rows(size, width)
    act_one, query, key, value = run(
        qkv_kernel, frames,
        [rows_bf, mod_row, whole((width, 3 * width)), whole((1, 3 * width)), by_rows(size, LANE), by_rows(size, LANE)],
        [rows_bf] * 4, [acts] * 4, (tokens, modulation, full_qkv, bias_qkv, cosine, sine), name="qkv",
    )
    pair = by_cols(count, LANE)
    table = whole((count, LANE))
    attended, aug = run(
        lambda *refs: attention_forward(*refs, frames=frames), width // LANE,
        [pair, pair, pair, table, table], [pair] * 2, [acts] * 2, (query, key, value, see, frame_hot), name="attf",
    )
    middle, attn, act_two = run(
        project_kernel, frames, [rows_bf, rows_bf, mod_row, whole((width, width)), row], [rows_bf] * 3,
        [wide, acts, acts], (attended, tokens, modulation, full_out, bias_out), name="proj",
    )
    full = whole((count, width))
    step = 512
    cols_h = by_cols(count, step)
    activated, slope = run(
        up_kernel, hidden // step, [full, by_cols(width, step), by_cols(1, step)], [cols_h] * 2, [tall] * 2,
        (act_two, full_up, bias_up), name="up",
    )
    acc = pltpu.VMEM((count, width), f32)
    block_out, d_branch, d_gate_two, bdown = run(
        down_kernel, hidden // width, [by_cols(count, width), by_rows(width, width), row, full, full, mod_all],
        [full, full, whole((frames, width)), row],
        [acts, acts, like((frames, width), f32), like((1, width), f32)],
        (activated, full_down, bias_down, middle, cotangent, modulation), [acc], name="down",
    )
    wdown = run(
        weight_grad_kernel, hidden // step, [cols_h, full], by_rows(step, width), like((hidden, width), bf16),
        (activated, d_branch), name="wdown",
    )
    wdown_grad = scatter(wdown)
    d_hidden, bup = run(
        hidden_back_kernel, hidden // step, [full, by_rows(step, width), cols_h], [cols_h, by_cols(1, step)],
        [tall, like((1, hidden), f32)], (d_branch, full_down, slope), name="dhid",
    )
    wup = run(
        weight_grad_kernel, hidden // step, [full, cols_h], by_cols(width, step), like((width, hidden), bf16),
        (act_two, d_hidden), name="wup",
    )
    wup_grad = scatter(wup)
    d_middle, d_attn, stat_two, bout = run(
        mlp_back_kernel, hidden // width,
        [by_cols(count, width), by_cols(width, width), full, full, full, mod_all],
        [full, full, whole((frames, 3, width)), row],
        [wide, acts, like((frames, 3, width), f32), like((1, width), f32)],
        (d_hidden, full_up, middle, cotangent, attn, modulation), [acc], name="dact2",
    )
    wout = run(
        weight_grad_kernel, width // step, [by_cols(count, step), full], by_rows(step, width), like((width, width), bf16),
        (attended, d_attn), name="wout",
    )
    wout_grad = scatter(wout)
    d_attended = dot(d_attn, full_out, NT).astype(bf16)
    d_projected, bqkv = run(
        lambda *refs: attention_backward(*refs, frames=frames), width // LANE, [pair] * 6 + [table] * 3,
        [pl.BlockSpec((3, count, LANE), lambda i: (0, 0, i)), pl.BlockSpec((1, 3, LANE), lambda i: (i, 0, 0))],
        [like((3, count, width), bf16), like((width // LANE, 3, LANE), f32)],
        (query, key, value, d_attended, attended, aug, see, cosine, sine), [pltpu.VMEM((count, LANE), f32)], name="attb",
    )
    stacked = pl.BlockSpec((1, count, width), lambda i: (i, 0, 0))
    wqkv = run(
        qkv_grad_kernel, 3, [full, stacked], by_cols(width, width), like((width, 3 * width), bf16),
        (act_one, d_projected), name="wqkv",
    )
    wqkv_grad = scatter(wqkv)
    token_grad, stat_one = run(
        input_back_kernel, 3, [stacked, by_cols(width, width), full, full, mod_all], [full, whole((frames, 2, width))],
        [acts, like((frames, 2, width), f32)], (d_projected, full_qkv, tokens, d_middle, modulation), [acc], name="dact1",
    )
    bqkv = jnp.transpose(bqkv, (1, 0, 2)).reshape(1, -1)
    sums = [bqkv, bout, bup, bdown]
    shares = [s.reshape(ndev, -1) for s in sums]
    packed = jnp.concatenate(shares, axis=1)
    bias_len = packed.shape[1]
    packed = jnp.pad(packed, ((0, 0), (0, -bias_len % LANE))).reshape(-1, LANE)
    bias_sum = scatter(packed).reshape(-1)[:bias_len]
    bias_grads, at = [], 0
    for share in shares:
        bias_grads.append(bias_sum[at : at + share.shape[1]])
        at += share.shape[1]
    d_modulation = jnp.concatenate(
        [stat_one[:, 0], stat_one[:, 1], stat_two[:, 0], stat_two[:, 1], stat_two[:, 2], d_gate_two], axis=1
    ).astype(bf16)
    d_mod = gather(d_modulation)
    wmod_grad = dot(cond, d_mod, TN)
    mine = b_mod.shape[0]
    bmod_grad = jnp.sum(lax.dynamic_slice(d_mod, (0, me * mine), (d_mod.shape[0], mine)).astype(f32), axis=0)
    gate = jax.nn.sigmoid(embedded)
    d_embed = dot(d_mod, w_mod, NT) * gate * (1.0 + embedded * (1.0 - gate))
    table_grad = lax.dot_general(
        d_embed, hot.astype(f32), TN, precision=lax.Precision.HIGHEST, preferred_element_type=f32
    )
    return (
        block_out, token_grad, wmod_grad, bmod_grad, wqkv_grad.astype(f32), bias_grads[0],
        wout_grad.astype(f32), bias_grads[1], wup_grad.astype(f32), bias_grads[2], wdown_grad.astype(f32),
        bias_grads[3], table_grad,
    )


def solution(mesh):
    rows, vec = P(AXES, None), P(AXES)
    return jax.shard_map(
        per_device,
        mesh=mesh,
        in_specs=(rows, rows, rows, vec, vec) + (rows, vec) * 5 + (rows,),
        out_specs=(rows, rows) + (rows, vec) * 5 + (rows,),
        check_vma=False,
    )
```

time: 2320 us -> 1230 us (0.53)
  matrix products: 588 us -> 11.5 us
  local copies, waits for them, and re-layouts: 353 us -> 11.7 us
  waiting for transfers between devices: 1070 us -> 823 us
  Pallas kernels: 0 us -> 226 us
  other arithmetic: 148 us -> 16.3 us
    dot_general x241 -> x6, matrix products: 588 us -> 11.5 us  [the longest x5 10.5 us: dot(): return lax.dot_general(left, right, dims, preferred_element_type=f32)]
    reduce_scatter x6 -> x4, waiting for transfers between devices: 952 us -> 518 us  [scatter(): return lax.psum_scatter(value, AXES, scatter_dimension=0, tiled=True)]
    pallas_call x0 -> x13, Pallas kernels: none -> 226 us  [run(): pl.pallas_call(kernel, grid=(grid,), in_specs=ins, out_specs=outs, out_sh...]
    squeeze x112 -> x0, local copies, waits for them, and re-layouts: 161 us -> none  [the longest x96 151 us: per_device(): lax.map(forward_head, (query_heads, key_heads, value_heads))]
    dynamic_update_slice x96 -> x0, local copies, waits for them, and re-layouts: 134 us -> none  [the longest x32 59 us: per_device(): lax.map(backward_head, (query_heads, key_heads, value_heads, grad_heads,...]
    all_gather x6 -> x5, waiting for transfers between devices: 119 us -> 217 us  [gather(): return lax.all_gather(value, AXES, axis=0, tiled=True)]
    unnamed x12 -> x11, waiting for transfers between devices: 3.73 us -> 87.9 us
    and x32 -> x0, other arithmetic: 71.2 us -> none  [per_device(): (clip_tok[:, None] == clip_tok[None, :]) & (frame_tok[None, :] <= frame_t...]
  transfers between devices with their start and end apart: 12 -> 10, of which waited for: 8 -> 9; matrix products, arithmetic and copies ran while one was open for 21% -> 2% of each run, Pallas kernels for 0% -> 9%
where the time goes in v1:
time: 1230 us
  waiting for transfers between devices  823 us (67%)
  Pallas kernels  226 us (18%)
  blocking collectives  123 us (10%)
  other arithmetic  16.3 us (1%)
  between operations  14.8 us (1%)
    reduce_scatter x4, waiting for transfers between devices, scatter(): return lax.psum_scatter(value, AXES, scatter_dimension=0, tiled=True)  518 us
    pallas_call x13, Pallas kernels, run(): pl.pallas_call(kernel, grid=(grid,), in_specs=ins, out_specs=outs, out_sh...  226 us
    all_gather x5, waiting for transfers between devices, gather(): return lax.all_gather(value, AXES, axis=0, tiled=True)  217 us
    unnamed x11, waiting for transfers between devices  87.9 us
    unnamed x2, blocking collectives  81.9 us
    all_gather x1, blocking collectives, gather(): return lax.all_gather(value, AXES, axis=0, tiled=True)  40.9 us
  transfers between devices with their start and end apart: 10, of which 9 were waited for; matrix products, arithmetic and copies ran while one was open for 2% of the time, Pallas kernels for 9%

profile of v1, /device:TPU:0, one launch (start us, length us, event | category | flops | bytes accessed | tf_op | source)
XLA Modules:
  0.0 1226.1 jit_solution(339673403847896812)
XLA Ops:
  7.3 0.9 dynamic-update-slice
  8.1 42.0 %all-reduce.2 = s32[128]{0:T(128)S(1)} all-reduce(s32[128]{0:T(128)S(1)} %dynamic-update-slice), channel_id=1, replica_groups=mesh['dp'=4,'fsdp'=8] {'dp','fsdp'}, use_global_device_ids=true, to_apply=%add.2 | all-reduce | flops 128 | bytes 1024
  50.1 1.1 fusion.2
  51.2 2.2 fusion.17
  53.6 0.7 all-gather.7.cloned.1.call-update
  54.4 0.7 all-gather.9.cloned.1.call-update
  55.1 0.5 all-gather.11.cloned.1.call-update
  55.7 0.5 all-gather.13.cloned.1.call-update
  56.5 0.2 select_reduce_fusion.4
  56.9 0.5 fusion.5
  57.4 0.2 copy.50
  57.7 0.2 copy.46
  58.0 40.9 %all_gather.22 = bf16[256,128]{1,0:T(8,128)(2,1)S(1)} all-gather(bf16[8,128]{1,0:T(8,128)(2,1)S(1)} %pad_bitcast_fusion), channel_id=1, replica_groups=mesh['dp'=4,'fsdp'=8] {'dp','fsdp'}, dimensions={0}, use_global_device_ids=true | all-gather | bytes 67584 | tf_op jit(solution)/shard_map/all_gather | solution.py:367
  99.1 0.7 reshape.147.b_ref
  99.9 0.7 reshape.148.b_ref
  100.6 0.6 copy.66
  101.2 0.7 reshape.150.b_ref
  102.0 1.8 pad_maximum_fusion
  103.8 0.9 compare_convert_fusion.refs_4_
  104.8 1.7 select_convert_fusion.refs_3_.refs_6_
  106.4 85.3 %all-reduce.7.cloned.1.call-done = f32[128,6144]{1,0:T(8,128)} async-done(((f32[128,6144]{1,0:T(8,128)}), f32[128,6144]{1,0:T(8,128)}) %all-reduce.7.cloned.1.call-update) | async-done | bytes 3145744
  191.8 1.0 dynamic-slice_add_fusion
  192.7 0.7 reshape.146.mod_ref
  193.5 69.4 %all-gather.7.cloned.1.call-done.w_ref = bf16[1024,3072]{1,0:T(8,128)(2,1)} async-done(((bf16[32,3072]{1,0:T(8,128)(2,1)}), bf16[1024,3072]{1,0:T(8,128)(2,1)}) %all-gather.7.cloned.1.call-update) | async-done | bytes 6291472 | tf_op jit(solution)/shard_map/all_gather | solution.py:367
  262.8 12.5 %qkv.1 = (bf16[1024,1024]{1,0:T(8,128)(2,1)}, bf16[1024,1024]{1,0:T(8,128)(2,1)}, bf16[1024,1024]{1,0:T(8,128)(2,1)}, bf16[1024,1024]{1,0:T(8,128)(2,1)}) custom-call(bf16[1024,1024]{1,0:T(8,128)(2,1)} %x_ref.5, f32[4,6,1024]{2,1,0:T(8,128)} %reshape.146.mod_ref, bf16[1024,3072]{1,0:T(8,128)(2,1)} %all-gather.7.cloned.1.call-done.w_ref, ...), custom_call_target="tpu_custom_call" | custom-call | bytes 19083264 | tf_op jit(solution)/shard_map/qkv/pallas_call | solution.py:305
  275.3 28.0 %attf.1 = (bf16[1024,1024]{1,0:T(8,128)(2,1)}, bf16[1024,1024]{1,0:T(8,128)(2,1)}) custom-call(bf16[1024,1024]{1,0:T(8,128)(2,1)} %get-tuple-element.38.refs_0_, bf16[1024,1024]{1,0:T(8,128)(2,1)} %get-tuple-element.39.refs_1_, bf16[1024,1024]{1,0:T(8,128)(2,1)} %get-tuple-element.40.refs_2_, bf16[1024,128]{1,0:T(8,128)(2,1)} %select_convert_fusion.refs_3_.refs_6_, ...), custom_call_target="tpu_custom_call" | custom-call | bytes 13631488 | tf_op jit(solution)/shard_map/attf/pallas_call | solution.py:305
  303.3 17.5 %all-gather.9.cloned.1.call-done.w_ref = bf16[1024,1024]{1,0:T(8,128)(2,1)} async-done(((bf16[32,1024]{1,0:T(8,128)(2,1)}), bf16[1024,1024]{1,0:T(8,128)(2,1)}) %all-gather.9.cloned.1.call-update) | async-done | bytes 2097168 | tf_op jit(solution)/shard_map/all_gather | solution.py:367
  320.8 8.1 proj.1
  328.8 70.7 %all-gather.11.cloned.1.call-done.w_ref = bf16[1024,4096]{1,0:T(8,128)(2,1)} async-done(((bf16[32,4096]{1,0:T(8,128)(2,1)}), bf16[1024,4096]{1,0:T(8,128)(2,1)}) %all-gather.11.cloned.1.call-update) | async-done | bytes 8388624 | tf_op jit(solution)/shard_map/all_gather | solution.py:367
  399.6 19.2 %up.1 = (bf16[1024,4096]{1,0:T(8,128)(2,1)}, bf16[1024,4096]{1,0:T(8,128)(2,1)}) custom-call(bf16[1024,1024]{1,0:T(8,128)(2,1)} %get-tuple-element.42.act_ref.left_ref, bf16[1024,4096]{1,0:T(8,128)(2,1)} %all-gather.11.cloned.1.call-done.w_ref, bf16[1,4096]{1,0:T(2,128)(2,1)} %bitcast.41), custom_call_target="tpu_custom_call" | custom-call | bytes 20987904 | tf_op jit(solution)/shard_map/up/pallas_call | solution.py:305
  418.8 59.4 %all-gather.13.cloned.1.call-done.w_ref = bf16[4096,1024]{1,0:T(8,128)(2,1)} async-done(((bf16[128,1024]{1,0:T(8,128)(2,1)}), bf16[4096,1024]{1,0:T(8,128)(2,1)}) %all-gather.13.cloned.1.call-update) | async-done | bytes 8388624 | tf_op jit(solution)/shard_map/all_gather | solution.py:367
  478.1 18.5 %down.1 = (bf16[1024,1024]{1,0:T(8,128)(2,1)}, bf16[1024,1024]{1,0:T(8,128)(2,1)}, f32[4,1024]{1,0:T(4,128)}, f32[1,1024]{1,0:T(1,128)}) custom-call(bf16[1024,4096]{1,0:T(8,128)(2,1)} %get-tuple-element.43.act_ref.left_ref, bf16[4096,1024]{1,0:T(8,128)(2,1)} %all-gather.13.cloned.1.call-done.w_ref, bf16[1,1024]{1,0:T(2,128)(2,1)} %reshape.150.b_ref, ...), custom_call_target="tpu_custom_call" | custom-call | bytes 46338048 | tf_op jit(solution)/shard_map/down/pallas_call | solution.py:305
  496.7 16.9 %dhid.1 = (bf16[1024,4096]{1,0:T(8,128)(2,1)}, f32[1,4096]{1,0:T(1,128)}) custom-call(bf16[1024,1024]{1,0:T(8,128)(2,1)} %get-tuple-element.46.dbr_ref.right_ref, bf16[4096,1024]{1,0:T(8,128)(2,1)} %all-gather.13.cloned.1.call-done.w_ref, bf16[1024,4096]{1,0:T(8,128)(2,1)} %get-tuple-element.47.slope_ref), custom_call_target="tpu_custom_call" | custom-call | bytes 37748736 | tf_op jit(solution)/shard_map/dhid/pallas_call | solution.py:305
  513.5 22.7 %dact2.1 = (f32[1024,1024]{1,0:T(8,128)}, bf16[1024,1024]{1,0:T(8,128)(2,1)}, f32[4,3,1024]{2,1,0:T(4,128)}, f32[1,1024]{1,0:T(1,128)}) custom-call(bf16[1024,4096]{1,0:T(8,128)(2,1)} %get-tuple-element.48.dh_ref.right_ref, bf16[1024,4096]{1,0:T(8,128)(2,1)} %all-gather.11.cloned.1.call-done.w_ref, f32[1024,1024]{1,0:T(8,128)} %get-tuple-element.44.mid_ref, ...), custom_call_target="tpu_custom_call" | custom-call | bytes 50528256 | tf_op jit(solution)/shard_map/dact2/pallas_call | solution.py:305
  536.3 5.3 convolution_convert_fusion.refs_3_
  541.6 37.6 %attb.1 = (bf16[3,1024,1024]{2,1,0:T(8,128)(2,1)}, f32[8,3,128]{2,1,0:T(4,128)}) custom-call(bf16[1024,1024]{1,0:T(8,128)(2,1)} %get-tuple-element.38.refs_0_, bf16[1024,1024]{1,0:T(8,128)(2,1)} %get-tuple-element.39.refs_1_, bf16[1024,1024]{1,0:T(8,128)(2,1)} %get-tuple-element.40.refs_2_, bf16[1024,1024]{1,0:T(8,128)(2,1)} %convolution_convert_fusion.refs_3_, ...), custom_call_target="tpu_custom_call" | custom-call | bytes 27787264 | tf_op jit(solution)/shard_map/attb/pallas_call | solution.py:305
  579.2 16.8 %dact1.1 = (bf16[1024,1024]{1,0:T(8,128)(2,1)}, f32[4,2,1024]{2,1,0:T(2,128)}) custom-call(bf16[3,1024,1024]{2,1,0:T(8,128)(2,1)} %get-tuple-element.52.dp_ref.right_ref, bf16[1024,3072]{1,0:T(8,128)(2,1)} %all-gather.7.cloned.1.call-done.w_ref, bf16[1024,1024]{1,0:T(8,128)(2,1)} %x_ref.5, f32[1024,1024]{1,0:T(8,128)} %get-tuple-element.53.dmid_ref, ...), custom_call_target="tpu_custom_call" | custom-call | bytes 37945344 | tf_op jit(solution)/shard_map/dact1/pallas_call | solution.py:305
  596.0 0.8 convert.23
  597.0 0.6 copy-done.2
  597.7 5.5 wout.1
  603.2 11.0 wqkv.1
  614.4 14.4 %wdown.1 = bf16[4096,1024]{1,0:T(8,128)(2,1)} custom-call(bf16[1024,4096]{1,0:T(8,128)(2,1)} %get-tuple-element.43.act_ref.left_ref, bf16[1024,1024]{1,0:T(8,128)(2,1)} %get-tuple-element.46.dbr_ref.right_ref), custom_call_target="tpu_custom_call" | custom-call | bytes 20971520 | tf_op jit(solution)/shard_map/wdown/pallas_call | solution.py:305
  628.8 14.5 %wup.1 = bf16[1024,4096]{1,0:T(8,128)(2,1)} custom-call(bf16[1024,1024]{1,0:T(8,128)(2,1)} %get-tuple-element.42.act_ref.left_ref, bf16[1024,4096]{1,0:T(8,128)(2,1)} %get-tuple-element.48.dh_ref.right_ref), custom_call_target="tpu_custom_call" | custom-call | bytes 20971520 | tf_op jit(solution)/shard_map/wup/pallas_call | solution.py:305
  643.4 0.7 copy-done.5
  644.1 0.5 broadcast.168
  644.6 0.7 reduce.7
  645.4 0.7 reduce.6
  646.2 39.9 %all-reduce.4 = f32[96,128]{1,0:T(8,128)S(1)} all-reduce(f32[96,128]{1,0:T(8,128)S(1)} %reshape.154), channel_id=4, replica_groups=mesh['dp'=4,'fsdp'=8] {'dp','fsdp'}, use_global_device_ids=true, to_apply=%region_10.11.clone | all-reduce | flops 12288 | bytes 98304
  686.1 0.5 slice.65
  686.7 0.5 slice_bitcast_fusion.1
  687.2 0.6 fusion.21
  687.8 2.7 reshape.160
  690.5 0.7 convert_reduce_fusion
  691.1 0.6 fusion
  691.8 1.0 fusion.1
  692.8 1.2 fusion.16
  694.0 97.1 %reduce-scatter.7.cloned.1.call-done = bf16[32,1024]{1,0:T(8,128)(2,1)} async-done(((bf16[1024,1024]{1,0:T(8,128)(2,1)}), bf16[32,1024]{1,0:T(8,128)(2,1)}) %reduce-scatter.7.cloned.1.call-update) | async-done | bytes 65552 | tf_op jit(solution)/shard_map/reduce_scatter | solution.py:370
  791.1 1.5 convert_element_type.73
  792.6 116.1 %reduce-scatter.5.cloned.1.call-done = bf16[32,3072]{1,0:T(8,128)(2,1)} async-done(((bf16[1024,3072]{1,0:T(8,128)(2,1)}), bf16[32,3072]{1,0:T(8,128)(2,1)}) %reduce-scatter.5.cloned.1.call-update) | async-done | bytes 196624 | tf_op jit(solution)/shard_map/reduce_scatter | solution.py:370
  908.7 1.7 convert_element_type.72
  910.4 153.7 %reduce-scatter.11.cloned.1.call-done = bf16[128,1024]{1,0:T(8,128)(2,1)} async-done(((bf16[4096,1024]{1,0:T(8,128)(2,1)}), bf16[128,1024]{1,0:T(8,128)(2,1)}) %reduce-scatter.11.cloned.1.call-update) | async-done | bytes 262160 | tf_op jit(solution)/shard_map/reduce_scatter | solution.py:370
  1064.1 1.8 convert_element_type.75
  1065.9 151.5 %reduce-scatter.9.cloned.1.call-done = bf16[32,4096]{1,0:T(8,128)(2,1)} async-done(((bf16[1024,4096]{1,0:T(8,128)(2,1)}), bf16[32,4096]{1,0:T(8,128)(2,1)}) %reduce-scatter.9.cloned.1.call-update) | async-done | bytes 262160 | tf_op jit(solution)/shard_map/reduce_scatter | solution.py:370
  1217.3 1.8 convert_element_type.74
  (88 shorter events, 2.1 us)
Async XLA Ops:
  7.2 44.0 %copy-start = (bf16[32,6144]{1,0:T(8,128)(2,1)S(1)}, bf16[32,6144]{1,0:T(8,128)(2,1)}, u32[]{:S(2)}) copy-start(bf16[32,6144]{1,0:T(8,128)(2,1)} %param.21) | copy-start | bytes 1179652
  7.2 184.6 %all-reduce.7.cloned.1.call-start = ((), (), s32[]{:S(2)}) async-start(), calls=%async_computation.13 | async-start | bytes 6291456
  53.5 2.8 copy-start.15
  53.5 4.4 copy-start.10
  53.5 4.4 copy-start.11
  53.5 4.4 copy-start.12
  53.5 4.4 copy-start.13
  53.5 4.4 copy-start.14
  53.6 209.3 %all-gather.7.cloned.1.call-start = ((), (), s32[]{:S(2)}) async-start(), calls=%async_computation.4 | async-start | bytes 6488064 | tf_op jit(solution)/shard_map/all_gather | solution.py:367
  54.3 266.4 %all-gather.9.cloned.1.call-start = ((), (), s32[]{:S(2)}) async-start(), calls=%async_computation.5 | async-start | bytes 2162688 | tf_op jit(solution)/shard_map/all_gather | solution.py:367
  55.0 344.5 %all-gather.11.cloned.1.call-start = ((), (), s32[]{:S(2)}) async-start(), calls=%async_computation.6 | async-start | bytes 8650752 | tf_op jit(solution)/shard_map/all_gather | solution.py:367
  55.6 422.5 %all-gather.13.cloned.1.call-start = ((), (), s32[]{:S(2)}) async-start(), calls=%async_computation.7 | async-start | bytes 8650752 | tf_op jit(solution)/shard_map/all_gather | solution.py:367
  56.2 631.5 %all-gather.15.cloned.1.call-start = ((), (), s32[]{:S(2)}) async-start(), calls=%async_computation.12 | async-start | bytes 1622016 | tf_op jit(solution)/shard_map/all_gather | solution.py:367
  57.7 46.2 %copy-start.7 = (s32[1024]{0:T(1024)S(1)}, s32[1024]{0:T(1024)}, u32[]{:S(2)}) copy-start(s32[1024]{0:T(1024)} %param.20) | copy-start | bytes 12292
  513.5 22.7 %copy-start.1 = (bf16[1024,1024]{1,0:T(8,128)(2,1)S(1)}, bf16[1024,1024]{1,0:T(8,128)(2,1)}, u32[]{:S(2)}) copy-start(bf16[1024,1024]{1,0:T(8,128)(2,1)} %all-gather.9.cloned.1.call-done.w_ref) | copy-start | bytes 6291460
  579.2 17.7 %copy-start.3 = (f32[4,3,1024]{2,1,0:T(4,128)S(1)}, f32[4,3,1024]{2,1,0:T(4,128)}, u32[]{:S(2)}) copy-start(f32[4,3,1024]{2,1,0:T(4,128)} %get-tuple-element.56) | copy-start | bytes 147460
  579.2 17.8 %copy-start.6 = (f32[4,1024]{1,0:T(4,128)S(1)}, f32[4,1024]{1,0:T(4,128)}, u32[]{:S(2)}) copy-start(f32[4,1024]{1,0:T(4,128)} %get-tuple-element.57) | copy-start | bytes 49156
  597.0 0.6 copy-start.2
  597.6 193.5 %reduce-scatter.7.cloned.1.call-start = ((), (), s32[]{:S(2)}) async-start(), calls=%async_computation.9 | async-start | bytes 2162688 | tf_op jit(solution)/shard_map/reduce_scatter | solution.py:370
  603.2 305.5 %reduce-scatter.5.cloned.1.call-start = ((), (), s32[]{:S(2)}) async-start(), calls=%async_computation.8 | async-start | bytes 6488064 | tf_op jit(solution)/shard_map/reduce_scatter | solution.py:370
  614.3 449.8 %reduce-scatter.11.cloned.1.call-start = ((), (), s32[]{:S(2)}) async-start(), calls=%async_computation.11 | async-start | bytes 8650752 | tf_op jit(solution)/shard_map/reduce_scatter | solution.py:370
  628.8 588.5 %reduce-scatter.9.cloned.1.call-start = ((), (), s32[]{:S(2)}) async-start(), calls=%async_computation.10 | async-start | bytes 8650752 | tf_op jit(solution)/shard_map/reduce_scatter | solution.py:370
  643.3 0.7 copy-start.5
  643.3 1.3 copy-start.9
  643.3 2.0 copy-start.8
  643.3 2.8 copy-start.4
Sparse Core Ops, SparseCore 0:
  53.6 138.1 all-reduce.6
  194.8 68.0 all-gather.6
  265.8 54.8 all-gather.8
  323.6 75.9 all-gather.10
  402.4 75.6 all-gather.12
  597.8 53.7 all-gather.14
  653.8 137.2 reduce-scatter.6
  796.7 111.9 reduce-scatter.4
  911.0 153.0 reduce-scatter.10
  1066.2 151.0 reduce-scatter.8

commit v2 on v1

--- a/solution.py
+++ b/solution.py
@@ -315,6 +315,315 @@
     )(*args)
 
 
+MESH = pl.DeviceIdType.MESH
+ANY = pl.BlockSpec(memory_space=pl.ANY)
+VMEM = pl.BlockSpec(memory_space=pltpu.VMEM)
+
+
+class Place:
+    def __init__(self, sizes):
+        self.sizes = sizes
+        self.ny, self.nx, self.nz = sizes
+        dp, fsdp = lax.axis_index("dp"), lax.axis_index("fsdp")
+        self.dp, self.fsdp = dp, fsdp
+        self.y, self.x = lax.div(dp, self.nx), lax.rem(dp, self.nx)
+        self.z, self.c = lax.div(fsdp, 2), lax.rem(fsdp, 2)
+
+    def shift(self, axis, k):
+        size = dict(y=self.ny, x=self.nx, z=self.nz, c=2)[axis]
+        return lax.rem(getattr(self, axis) + (k + size), size)
+
+    def device(self, axis, k):
+        at = self.shift(axis, k)
+        if axis == "y":
+            return (at * self.nx + self.x, self.fsdp)
+        if axis == "x":
+            return (self.y * self.nx + at, self.fsdp)
+        if axis == "z":
+            return (self.dp, at * 2 + self.c)
+        return (self.dp, self.z * 2 + at)
+
+    def peers(self):
+        for axis, size in zip("yxzc", (self.ny, self.nx, self.nz, 2)):
+            for k in range(1, size):
+                yield axis, k
+
+    def enter(self):
+        barrier = pltpu.get_barrier_semaphore()
+        peers = list(self.peers())
+        for axis, k in peers:
+            pl.semaphore_signal(barrier, inc=1, device_id=self.device(axis, k), device_id_type=MESH)
+        pl.semaphore_wait(barrier, len(peers))
+
+
+class Links:
+    def __init__(self, place, send, recv):
+        self.place, self.send, self.recv = place, send, recv
+        self.slots, self.sent = {}, []
+
+    def copy(self, key, src, dst, axis, k):
+        slot = self.slots.setdefault(key, len(self.slots))
+        return pltpu.make_async_remote_copy(
+            src_ref=src, dst_ref=dst, send_sem=self.send.at[slot], recv_sem=self.recv.at[slot],
+            device_id=self.place.device(axis, k), device_id_type=MESH,
+        )
+
+    def start(self, key, src, dst, axis, k):
+        self.copy(key, src, dst, axis, k).start()
+        self.sent.append((key, src, dst, axis, k))
+
+    def arrived(self, key, dst, axis, k):
+        self.copy(key, dst, dst, axis, k).wait_recv()
+
+    def drain(self):
+        for item in self.sent:
+            self.copy(*item).wait_send()
+
+
+class Gather:
+    phases = 5
+
+    @staticmethod
+    def copies(sizes):
+        ny, nx, nz = sizes
+        return (nz - 1) + 2 * (nx - 1) + 2 * (ny - 1) + 1 + 2 * (nx - 1) + 2 * (ny - 1)
+
+    def __init__(self, place, shard, full, send, recv, local):
+        self.place, self.shard, self.full, self.local = place, shard, full, local
+        self.links = Links(place, send, recv)
+        half = place.nz // 2
+        self.low, self.high = pl.ds(0, half), pl.ds(half, place.nz - half)
+
+    def own(self):
+        p = self.place
+        return pltpu.make_async_copy(self.shard, self.full.at[p.y, p.x, p.z, p.c], self.local.at[0])
+
+    def send(self, key, ref, axis, k):
+        self.links.start(key, ref, ref, axis, k)
+
+    def phase(self, step):
+        p, full = self.place, self.full
+        y, x, z, c = p.y, p.x, p.z, p.c
+        if step == 0:
+            self.own().start()
+            for k in range(1, p.nz):
+                self.links.start(("z", k), self.shard, full.at[y, x, z, c], "z", k)
+        elif step == 1:
+            self.own().wait()
+            for k in range(1, p.nz):
+                self.links.arrived(("z", k), full.at[y, x, p.shift("z", -k), c], "z", k)
+            for k in range(1, p.nx):
+                self.send(("x", k), full.at[y, x, self.low, c], "x", k)
+            for k in range(1, p.ny):
+                self.send(("y", k), full.at[y, x, self.high, c], "y", k)
+            self.send("c", full.at[y, x, :, c], "c", 1)
+        elif step == 2:
+            for k in range(1, p.nx):
+                self.links.arrived(("x", k), full.at[y, p.shift("x", -k), self.low, c], "x", k)
+            for k in range(1, p.ny):
+                self.links.arrived(("y", k), full.at[p.shift("y", -k), x, self.high, c], "y", k)
+            for k in range(1, p.ny):
+                self.send(("xy", k), full.at[y, :, self.low, c], "y", k)
+            for k in range(1, p.nx):
+                self.send(("yx", k), full.at[:, x, self.high, c], "x", k)
+            for k in range(1, p.nx):
+                self.send(("cx", k), full.at[y, p.shift("x", -k), self.low, c], "c", 1)
+            for k in range(1, p.ny):
+                self.send(("cy", k), full.at[p.shift("y", -k), x, self.high, c], "c", 1)
+        elif step == 3:
+            for k in range(1, p.ny):
+                ref = full.at[p.shift("y", -k), :, self.low, c]
+                self.links.arrived(("xy", k), ref, "y", k)
+                self.send(("cxy", k), ref, "c", 1)
+            for k in range(1, p.nx):
+                ref = full.at[:, p.shift("x", -k), self.high, c]
+                self.links.arrived(("yx", k), ref, "x", k)
+                self.send(("cyx", k), ref, "c", 1)
+        else:
+            d = 1 - c
+            self.links.arrived("c", full.at[y, x, :, d], "c", 1)
+            for k in range(1, p.nx):
+                self.links.arrived(("cx", k), full.at[y, p.shift("x", -k), self.low, d], "c", 1)
+                self.links.arrived(("cyx", k), full.at[:, p.shift("x", -k), self.high, d], "c", 1)
+            for k in range(1, p.ny):
+                self.links.arrived(("cy", k), full.at[p.shift("y", -k), x, self.high, d], "c", 1)
+                self.links.arrived(("cxy", k), full.at[p.shift("y", -k), :, self.low, d], "c", 1)
+            self.links.drain()
+
+
+class Reduce:
+    phases = 5
+
+    @staticmethod
+    def copies(sizes):
+        ny, nx, nz = sizes
+        return 1 + 2 * (nx - 1) + 2 * (ny - 1) + (nz - 1)
+
+    @staticmethod
+    def scratch(sizes, block, kind):
+        ny, nx, nz = sizes
+        half = nz // 2
+        rest = nz - half
+        return [
+            pltpu.VMEM((ny, nx, nz) + block, kind),
+            pltpu.VMEM((ny, nx, nz) + block, kind),
+            pltpu.VMEM((ny - 1, nx, half) + block, kind),
+            pltpu.VMEM((nx - 1, ny, rest) + block, kind),
+            pltpu.VMEM((nx - 1, half) + block, kind),
+            pltpu.VMEM((ny - 1, rest) + block, kind),
+            pltpu.VMEM((nz - 1,) + block, kind),
+        ]
+
+    def __init__(self, place, source, out, bufs, send, recv, local):
+        self.place, self.source, self.out, self.local = place, source, out, local
+        self.acc, self.core, self.la, self.lb, self.ma, self.mb, self.last = bufs
+        self.links = Links(place, send, recv)
+        self.half = place.nz // 2
+        self.low, self.high = pl.ds(0, self.half), pl.ds(self.half, place.nz - self.half)
+
+    def own(self):
+        p = self.place
+        return pltpu.make_async_copy(self.source.at[:, :, :, p.c], self.acc, self.local.at[0])
+
+    def add(self, counts, into, terms):
+        total = 1
+        for n in counts:
+            total *= n
+
+        def body(flat, carry):
+            at = []
+            for n in reversed(counts):
+                at.append(lax.rem(flat, n))
+                flat = lax.div(flat, n)
+            at = at[::-1]
+            where = into(*at)
+            value = self.acc[where].astype(f32)
+            for ref, index in terms(*at):
+                value = value + ref[index].astype(f32)
+            self.acc[where] = value.astype(self.acc.dtype)
+            return carry
+
+        lax.fori_loop(0, total, body, 0)
+
+    def phase(self, step):
+        p, acc = self.place, self.acc
+        y, x, z, c = p.y, p.x, p.z, p.c
+        half, rest = self.half, p.nz - self.half
+        if step == 0:
+            self.own().start()
+            self.links.start("c", self.source.at[:, :, :, 1 - c], self.core, "c", 1)
+        elif step == 1:
+            self.own().wait()
+            self.links.arrived("c", self.core, "c", 1)
+            self.add((p.ny, p.nx, p.nz), lambda *at: at, lambda *at: [(self.core, at)])
+            for k in range(1, p.ny):
+                self.links.start(("y", k), acc.at[p.shift("y", k), :, self.low], self.la.at[k - 1], "y", k)
+            for k in range(1, p.nx):
+                self.links.start(("x", k), acc.at[:, p.shift("x", k), self.high], self.lb.at[k - 1], "x", k)
+        elif step == 2:
+            for k in range(1, p.ny):
+                self.links.arrived(("y", k), self.la.at[k - 1], "y", k)
+            self.add(
+                (p.nx, half), lambda i, j: (y, i, j),
+                lambda i, j: [(self.la, (k, i, j)) for k in range(p.ny - 1)],
+            )
+            for k in range(1, p.nx):
+                self.links.start(("yx", k), acc.at[y, p.shift("x", k), self.low], self.ma.at[k - 1], "x", k)
+            for k in range(1, p.nx):
+                self.links.arrived(("x", k), self.lb.at[k - 1], "x", k)
+            self.add(
+                (p.ny, rest), lambda i, j: (i, x, half + j),
+                lambda i, j: [(self.lb, (k, i, j)) for k in range(p.nx - 1)],
+            )
+            for k in range(1, p.ny):
+                self.links.start(("xy", k), acc.at[p.shift("y", k), x, self.high], self.mb.at[k - 1], "y", k)
+        elif step == 3:
+            for k in range(1, p.nx):
+                self.links.arrived(("yx", k), self.ma.at[k - 1], "x", k)
+            for k in range(1, p.ny):
+                self.links.arrived(("xy", k), self.mb.at[k - 1], "y", k)
+            self.add((half,), lambda j: (y, x, j), lambda j: [(self.ma, (k, j)) for k in range(p.nx - 1)])
+            self.add((rest,), lambda j: (y, x, half + j), lambda j: [(self.mb, (k, j)) for k in range(p.ny - 1)])
+            for k in range(1, p.nz):
+                self.links.start(("z", k), acc.at[y, x, p.shift("z", k)], self.last.at[k - 1], "z", k)
+        else:
+            for k in range(1, p.nz):
+                self.links.arrived(("z", k), self.last.at[k - 1], "z", k)
+            value = acc[y, x, z].astype(f32)
+            for k in range(p.nz - 1):
+                value = value + self.last[k].astype(f32)
+            self.out[...] = value
+            self.links.drain()
+
+
+class Transfers:
+    def __init__(self, sizes, gathers=(), reduces=()):
+        self.sizes = sizes
+        self.gathers, self.reduces = list(gathers), list(reduces)
+        ny, nx, nz = sizes
+        self.lead = (ny, nx, nz, 2)
+        blocks = [(r.shape[0] // (ny * nx * nz * 2), r.shape[1]) for r in self.reduces]
+        self.args = self.gathers + [r.reshape(self.lead + b) for r, b in zip(self.reduces, blocks)]
+        self.in_specs = [VMEM] * len(self.gathers) + [ANY] * len(self.reduces)
+        self.out_specs = [ANY] * len(self.gathers) + [VMEM] * len(self.reduces)
+        self.shapes = [like(self.lead + g.shape, g.dtype) for g in self.gathers]
+        self.shapes += [like(b, f32) for b in blocks]
+        self.scratch = []
+        for _ in self.gathers:
+            self.scratch += [pltpu.SemaphoreType.DMA((Gather.copies(sizes),))] * 2
+            self.scratch += [pltpu.SemaphoreType.DMA((1,))]
+        for r, b in zip(self.reduces, blocks):
+            self.scratch += Reduce.scratch(sizes, b, r.dtype)
+            self.scratch += [pltpu.SemaphoreType.DMA((Reduce.copies(sizes),))] * 2
+            self.scratch += [pltpu.SemaphoreType.DMA((1,))]
+
+    def build(self, ins, outs, scratch):
+        place = Place(self.sizes)
+        scratch = list(scratch)
+        count = len(self.gathers)
+        tasks = []
+        for i in range(count):
+            tasks.append(Gather(place, ins[i], outs[i], *scratch[3 * i : 3 * i + 3]))
+        scratch = scratch[3 * count :]
+        for i in range(len(self.reduces)):
+            part = scratch[10 * i : 10 * i + 10]
+            tasks.append(Reduce(place, ins[count + i], outs[count + i], part[:7], *part[7:]))
+        return place, tasks
+
+    def finish(self, outs):
+        whole_outs = []
+        for out, gathered in zip(outs, self.gathers):
+            whole_outs.append(out.reshape((-1,) + gathered.shape[1:]))
+        return whole_outs + list(outs[len(self.gathers) :])
+
+
+def exchange(transfers, order, name, collective_id):
+    def body(*refs):
+        n_in, n_out = len(transfers.args), len(transfers.shapes)
+        place, tasks = transfers.build(refs[:n_in], refs[n_in : n_in + n_out], refs[n_in + n_out :])
+        place.enter()
+        for task, step in order:
+            tasks[task].phase(step)
+
+    outs = pl.pallas_call(
+        body,
+        in_specs=transfers.in_specs,
+        out_specs=transfers.out_specs,
+        out_shape=transfers.shapes,
+        scratch_shapes=transfers.scratch,
+        name=name,
+        compiler_params=pltpu.CompilerParams(
+            vmem_limit_bytes=60 * 1024 * 1024, collective_id=collective_id, has_side_effects=True
+        ),
+    )(*transfers.args)
+    return transfers.finish(outs)
+
+
+def staggered(starts, phases=5):
+    turns = [(s + p, i, p) for i, s in enumerate(starts) for p in range(phases)]
+    return [(i, p) for _, i, p in sorted(turns)]
+
+
 def tables(clip_row, pad, count):
     frames = clip_row.shape[0]
     size = count // frames
@@ -363,29 +672,30 @@
     ndev = width // w_up.shape[0]
     me = lax.axis_index("dp") * lax.axis_size("fsdp") + lax.axis_index("fsdp")
 
-    def gather(value):
-        return lax.all_gather(value, AXES, axis=0, tiled=True)
-
-    def scatter(value):
-        return lax.psum_scatter(value, AXES, scatter_dimension=0, tiled=True)
-
-    all_levels = gather(levels)
+    dp, fsdp = lax.axis_size("dp"), lax.axis_size("fsdp")
+    sizes = (dp // 2, 2, fsdp // 2)
+
+    biases = [b_mod, b_qkv, b_out, b_up, b_down]
+    lengths = [b.shape[0] for b in biases]
+    packed = jnp.concatenate([levels.astype(f32)] + [b.astype(f32) for b in biases])
+    packed = jnp.pad(packed, (0, 8 * LANE - packed.shape[0])).reshape(8, LANE)
+    small, full_qkv = exchange(Transfers(sizes, [packed, w_qkv]), staggered([0, 0]), "gather_in", 1)
+    small = small.reshape(ndev, -1)
+    all_levels = small[:, :frames].reshape(-1).astype(jnp.int32)
+    full_bias, at = [], frames
+    for length in lengths:
+        full_bias.append(small[:, at : at + length].reshape(1, -1))
+        at += length
+    bias_mod, bias_qkv, bias_out, bias_up, bias_down = full_bias
+
     hot = (all_levels[:, None] == jnp.arange(noise_table.shape[1], dtype=jnp.int32)[None, :]).astype(bf16)
     embedded = dot(hot, noise_table, NT)
     cond = jax.nn.silu(embedded).astype(bf16)
     partial = dot(cond, w_mod, NN)
-    biases = [b_mod, b_qkv, b_out, b_up, b_down]
-    lengths = [b.shape[0] for b in biases]
-    packed = jnp.concatenate(biases)
-    packed = jnp.pad(packed, (0, -packed.shape[0] % (8 * LANE))).reshape(8, -1)
-    packed = gather(packed).reshape(ndev, -1)
-    full_bias, at = [], 0
-    for length in lengths:
-        full_bias.append(packed[:, at : at + length].reshape(1, -1))
-        at += length
-    bias_mod, bias_qkv, bias_out, bias_up, bias_down = full_bias
-    modulation = (scatter(partial) + bias_mod.astype(f32)).reshape(frames, 6, width)
-    full_qkv, full_out, full_up, full_down = gather(w_qkv), gather(w_out), gather(w_up), gather(w_down)
+    full_out, full_up, full_down, modulation = exchange(
+        Transfers(sizes, [w_out, w_up, w_down], [partial.reshape(ndev * 8, -1)]), staggered([1, 2, 3, 0]), "gather_mod", 2
+    )
+    modulation = (modulation.reshape(frames, -1) + bias_mod).reshape(frames, 6, width)
     see, frame_hot, cosine, sine = tables(clip_frames[0], pad_mask, count)
 
     acts = like((count, width), bf16)
@@ -428,7 +738,6 @@
         weight_grad_kernel, hidden // step, [cols_h, full], by_rows(step, width), like((hidden, width), bf16),
         (activated, d_branch), name="wdown",
     )
-    wdown_grad = scatter(wdown)
     d_hidden, bup = run(
         hidden_back_kernel, hidden // step, [full, by_rows(step, width), cols_h], [cols_h, by_cols(1, step)],
         [tall, like((1, hidden), f32)], (d_branch, full_down, slope), name="dhid",
@@ -437,7 +746,6 @@
         weight_grad_kernel, hidden // step, [full, cols_h], by_cols(width, step), like((width, hidden), bf16),
         (act_two, d_hidden), name="wup",
     )
-    wup_grad = scatter(wup)
     d_middle, d_attn, stat_two, bout = run(
         mlp_back_kernel, hidden // width,
         [by_cols(count, width), by_cols(width, width), full, full, full, mod_all],
@@ -449,7 +757,6 @@
         weight_grad_kernel, width // step, [by_cols(count, step), full], by_rows(step, width), like((width, width), bf16),
         (attended, d_attn), name="wout",
     )
-    wout_grad = scatter(wout)
     d_attended = dot(d_attn, full_out, NT).astype(bf16)
     d_projected, bqkv = run(
         lambda *refs: attention_backward(*refs, frames=frames), width // LANE, [pair] * 6 + [table] * 3,
@@ -462,26 +769,29 @@
         qkv_grad_kernel, 3, [full, stacked], by_cols(width, width), like((width, 3 * width), bf16),
         (act_one, d_projected), name="wqkv",
     )
-    wqkv_grad = scatter(wqkv)
     token_grad, stat_one = run(
         input_back_kernel, 3, [stacked, by_cols(width, width), full, full, mod_all], [full, whole((frames, 2, width))],
         [acts, like((frames, 2, width), f32)], (d_projected, full_qkv, tokens, d_middle, modulation), [acc], name="dact1",
     )
     bqkv = jnp.transpose(bqkv, (1, 0, 2)).reshape(1, -1)
     sums = [bqkv, bout, bup, bdown]
-    shares = [s.reshape(ndev, -1) for s in sums]
+    shares = [b.reshape(ndev, -1) for b in sums]
     packed = jnp.concatenate(shares, axis=1)
     bias_len = packed.shape[1]
-    packed = jnp.pad(packed, ((0, 0), (0, -bias_len % LANE))).reshape(-1, LANE)
-    bias_sum = scatter(packed).reshape(-1)[:bias_len]
+    packed = jnp.pad(packed, ((0, 0), (0, 8 * LANE - bias_len))).reshape(-1, LANE)
+    d_modulation = jnp.concatenate(
+        [stat_one[:, 0], stat_one[:, 1], stat_two[:, 0], stat_two[:, 1], stat_two[:, 2], d_gate_two], axis=1
+    ).astype(bf16)
+    d_mod, bias_sum, wdown_grad, wup_grad, wqkv_grad, wout_grad = exchange(
+        Transfers(sizes, [d_modulation.reshape(16, -1)], [packed, wdown, wup, wqkv, wout]),
+        staggered([0, 0, 0, 1, 2, 3]), "reduce", 3,
+    )
+    d_mod = d_mod.reshape(ndev * frames, -1)
+    bias_sum = bias_sum.reshape(-1)[:bias_len]
     bias_grads, at = [], 0
     for share in shares:
         bias_grads.append(bias_sum[at : at + share.shape[1]])
         at += share.shape[1]
-    d_modulation = jnp.concatenate(
-        [stat_one[:, 0], stat_one[:, 1], stat_two[:, 0], stat_two[:, 1], stat_two[:, 2], d_gate_two], axis=1
-    ).astype(bf16)
-    d_mod = gather(d_modulation)
     wmod_grad = dot(cond, d_mod, TN)
     mine = b_mod.shape[0]
     bmod_grad = jnp.sum(lax.dynamic_slice(d_mod, (0, me * mine), (d_mod.shape[0], mine)).astype(f32), axis=0)
@@ -491,8 +801,8 @@
         d_embed, hot.astype(f32), TN, precision=lax.Precision.HIGHEST, preferred_element_type=f32
     )
     return (
-        block_out, token_grad, wmod_grad, bmod_grad, wqkv_grad.astype(f32), bias_grads[0],
-        wout_grad.astype(f32), bias_grads[1], wup_grad.astype(f32), bias_grads[2], wdown_grad.astype(f32),
+        block_out, token_grad, wmod_grad, bmod_grad, wqkv_grad, bias_grads[0],
+        wout_grad, bias_grads[1], wup_grad, bias_grads[2], wdown_grad,
         bias_grads[3], table_grad,
     )
 

time: 1230 us -> 583 us (0.47)
  waiting for transfers between devices: 823 us -> 0 us
  Pallas kernels: 226 us -> 536 us
  blocking collectives: 123 us -> 0 us
  between operations: 14.8 us -> 1.42 us
    reduce_scatter x4 -> x0, waiting for transfers between devices: 518 us -> none  [scatter(): return lax.psum_scatter(value, AXES, scatter_dimension=0, tiled=True)]
    pallas_call x0 -> x3, Pallas kernels: none -> 311 us  [exchange(): pl.pallas_call(body, in_specs=transfers.in_specs, out_specs=transfers.out...]
    all_gather x5 -> x0, waiting for transfers between devices: 217 us -> none  [gather(): return lax.all_gather(value, AXES, axis=0, tiled=True)]
    unnamed x11 -> x0, waiting for transfers between devices: 87.9 us -> none
    unnamed x2 -> x0, blocking collectives: 81.9 us -> none
    all_gather x1 -> x0, blocking collectives: 40.9 us -> none  [gather(): return lax.all_gather(value, AXES, axis=0, tiled=True)]
  transfers between devices with their start and end apart: 10 -> 0, of which waited for: 9 -> 0; matrix products, arithmetic and copies ran while one was open for 2% -> 0% of each run, Pallas kernels for 9% -> 0%
where the time goes in v2:
time: 583 us; the launch traced here: 579 us
  Pallas kernels  536 us (92%)
  local copies, waits for them, and re-layouts  21.5 us (4%)
  other arithmetic  11 us (2%)
  matrix products  8.99 us (2%)
    pallas_call x3, Pallas kernels, exchange(): pl.pallas_call(body, in_specs=transfers.in_specs, out_specs=transfers.out...  311 us
    pallas_call x13, Pallas kernels, run(): pl.pallas_call(kernel, grid=(grid,), in_specs=ins, out_specs=outs, out_sh...  225 us

profile of v2, /device:TPU:0, one launch (start us, length us, event | category | flops | bytes accessed | tf_op | source)
XLA Modules:
  0.0 578.8 jit_solution(17126173741046744557)
XLA Ops:
  0.7 0.8 select_reduce_fusion.5
  1.5 0.1 convert_reduce_fusion.1
  1.6 0.7 fusion.16
  2.3 0.2 select_reduce_fusion.4
  2.5 0.7 select_reduce_fusion
  3.2 0.1 broadcast_multiply_fusion.1
  3.3 0.5 fusion.6
  3.8 0.2 copy.50
  4.1 0.2 copy.46
  4.3 1.9 pad_maximum_fusion
  6.2 0.1 concatenate.19
  6.3 0.6 pad_bitcast_fusion.refs_0_
  6.9 52.7 %gather_in.1 = (f32[2,2,4,2,8,128]{5,4,3,2,1,0:T(8,128)}, bf16[2,2,4,2,32,3072]{5,4,3,2,1,0:T(8,128)(2,1)}) custom-call(f32[8,128]{1,0:T(8,128)} %pad_bitcast_fusion.refs_0_, bf16[32,3072]{1,0:T(8,128)(2,1)} %refs_1_.2), custom_call_target="tpu_custom_call" | custom-call | tf_op jit(solution)/shard_map/gather_in/pallas_call | solution.py:608
  59.6 0.9 copy.67
  60.6 0.6 copy-done.4
  61.2 0.1 convert_element_type.78
  61.3 0.5 copy-done.20
  61.8 0.3 fusion.2
  62.1 0.6 fusion.18
  62.7 2.4 reshape_reshape.16.refs_3_
  65.2 107.4 %gather_mod.1 = (bf16[2,2,4,2,32,1024]{5,4,3,2,1,0:T(8,128)(2,1)}, bf16[2,2,4,2,32,4096]{5,4,3,2,1,0:T(8,128)(2,1)}, bf16[2,2,4,2,128,1024]{5,4,3,2,1,0:T(8,128)(2,1)}, f32[8,3072]{1,0:T(8,128)}) custom-call(bf16[32,1024]{1,0:T(8,128)(2,1)} %refs_0_.1, bf16[32,4096]{1,0:T(8,128)(2,1)} %refs_1_.3, bf16[128,1024]{1,0:T(8,128)(2,1)} %refs_2_.1, ...), custom_call_target="tpu_custom_call" | custom-call | tf_op jit(solution)/shard_map/gather_mod/pallas_call | solution.py:608
  172.5 0.9 reshape.171
  173.5 0.1 add.68
  173.6 0.7 broadcast_add_fusion.mod_ref
  174.4 0.7 reshape.173.b_ref
  175.1 12.5 %qkv.1 = (bf16[1024,1024]{1,0:T(8,128)(2,1)}, bf16[1024,1024]{1,0:T(8,128)(2,1)}, bf16[1024,1024]{1,0:T(8,128)(2,1)}, bf16[1024,1024]{1,0:T(8,128)(2,1)}) custom-call(bf16[1024,1024]{1,0:T(8,128)(2,1)} %x_ref.5, f32[4,6,1024]{2,1,0:T(8,128)} %broadcast_add_fusion.mod_ref, bf16[1024,3072]{1,0:T(8,128)(2,1)} %bitcast.59, f32[1,3072]{1,0:T(1,128)} %reshape.173.b_ref, ...), custom_call_target="tpu_custom_call" | custom-call | bytes 19095552 | tf_op jit(solution)/shard_map/qkv/pallas_call | solution.py:305
  187.6 0.1 select_reduce_fusion.3
  187.8 1.5 select_convert_fusion.refs_3_.refs_6_
  189.3 0.9 compare_convert_fusion.refs_4_
  190.2 27.9 %attf.1 = (bf16[1024,1024]{1,0:T(8,128)(2,1)}, bf16[1024,1024]{1,0:T(8,128)(2,1)}) custom-call(bf16[1024,1024]{1,0:T(8,128)(2,1)} %get-tuple-element.53.refs_0_, bf16[1024,1024]{1,0:T(8,128)(2,1)} %get-tuple-element.54.refs_1_, bf16[1024,1024]{1,0:T(8,128)(2,1)} %get-tuple-element.55.refs_2_, bf16[1024,128]{1,0:T(8,128)(2,1)} %select_convert_fusion.refs_3_.refs_6_, ...), custom_call_target="tpu_custom_call" | custom-call | bytes 13631488 | tf_op jit(solution)/shard_map/attf/pallas_call | solution.py:305
  218.2 0.7 reshape.175.b_ref
  218.9 8.0 %proj.1 = (f32[1024,1024]{1,0:T(8,128)}, bf16[1024,1024]{1,0:T(8,128)(2,1)}, bf16[1024,1024]{1,0:T(8,128)(2,1)}) custom-call(bf16[1024,1024]{1,0:T(8,128)(2,1)} %get-tuple-element.56.att_ref.refs_4_.left_ref, bf16[1024,1024]{1,0:T(8,128)(2,1)} %x_ref.5, f32[4,6,1024]{2,1,0:T(8,128)} %broadcast_add_fusion.mod_ref, bf16[1024,1024]{1,0:T(8,128)(2,1)} %bitcast.62, ...), custom_call_target="tpu_custom_call" | custom-call | bytes 12787712 | tf_op jit(solution)/shard_map/proj/pallas_call | solution.py:305
  226.9 0.7 slice.78
  227.6 19.2 %up.1 = (bf16[1024,4096]{1,0:T(8,128)(2,1)}, bf16[1024,4096]{1,0:T(8,128)(2,1)}) custom-call(bf16[1024,1024]{1,0:T(8,128)(2,1)} %get-tuple-element.58.act_ref.left_ref, bf16[1024,4096]{1,0:T(8,128)(2,1)} %bitcast.52, f32[1,4096]{1,0:T(1,128)} %bitcast.71), custom_call_target="tpu_custom_call" | custom-call | bytes 21004288 | tf_op jit(solution)/shard_map/up/pallas_call | solution.py:305
  246.8 0.7 reshape.179.b_ref
  247.4 18.7 %down.1 = (bf16[1024,1024]{1,0:T(8,128)(2,1)}, bf16[1024,1024]{1,0:T(8,128)(2,1)}, f32[4,1024]{1,0:T(4,128)}, f32[1,1024]{1,0:T(1,128)}) custom-call(bf16[1024,4096]{1,0:T(8,128)(2,1)} %get-tuple-element.60.act_ref.left_ref, bf16[4096,1024]{1,0:T(8,128)(2,1)} %bitcast.54, f32[1,1024]{1,0:T(1,128)} %reshape.179.b_ref, ...), custom_call_target="tpu_custom_call" | custom-call | bytes 46342144 | tf_op jit(solution)/shard_map/down/pallas_call | solution.py:305
  266.2 16.7 %dhid.1 = (bf16[1024,4096]{1,0:T(8,128)(2,1)}, f32[1,4096]{1,0:T(1,128)}) custom-call(bf16[1024,1024]{1,0:T(8,128)(2,1)} %get-tuple-element.64.dbr_ref.right_ref, bf16[4096,1024]{1,0:T(8,128)(2,1)} %bitcast.55, bf16[1024,4096]{1,0:T(8,128)(2,1)} %get-tuple-element.65.slope_ref), custom_call_target="tpu_custom_call" | custom-call | bytes 37748736 | tf_op jit(solution)/shard_map/dhid/pallas_call | solution.py:305
  282.8 22.6 %dact2.1 = (f32[1024,1024]{1,0:T(8,128)}, bf16[1024,1024]{1,0:T(8,128)(2,1)}, f32[4,3,1024]{2,1,0:T(4,128)}, f32[1,1024]{1,0:T(1,128)}) custom-call(bf16[1024,4096]{1,0:T(8,128)(2,1)} %get-tuple-element.66.dh_ref.right_ref, bf16[1024,4096]{1,0:T(8,128)(2,1)} %bitcast.53, f32[1024,1024]{1,0:T(8,128)} %get-tuple-element.62.mid_ref, ...), custom_call_target="tpu_custom_call" | custom-call | bytes 50528256 | tf_op jit(solution)/shard_map/dact2/pallas_call | solution.py:305
  305.4 6.0 %wout.1 = bf16[1024,1024]{1,0:T(8,128)(2,1)} custom-call(bf16[1024,1024]{1,0:T(8,128)(2,1)} %get-tuple-element.56.att_ref.refs_4_.left_ref, bf16[1024,1024]{1,0:T(8,128)(2,1)} %get-tuple-element.68.right_ref), custom_call_target="tpu_custom_call" | custom-call | bytes 8388608 | tf_op jit(solution)/shard_map/wout/pallas_call | solution.py:305
  311.4 5.3 convolution_convert_fusion.refs_3_
  316.7 37.2 %attb.1 = (bf16[3,1024,1024]{2,1,0:T(8,128)(2,1)}, f32[8,3,128]{2,1,0:T(4,128)}) custom-call(bf16[1024,1024]{1,0:T(8,128)(2,1)} %get-tuple-element.53.refs_0_, bf16[1024,1024]{1,0:T(8,128)(2,1)} %get-tuple-element.54.refs_1_, bf16[1024,1024]{1,0:T(8,128)(2,1)} %get-tuple-element.55.refs_2_, bf16[1024,1024]{1,0:T(8,128)(2,1)} %convolution_convert_fusion.refs_3_, ...), custom_call_target="tpu_custom_call" | custom-call | bytes 27787264 | tf_op jit(solution)/shard_map/attb/pallas_call | solution.py:305
  353.9 10.7 %wqkv.1 = bf16[1024,3072]{1,0:T(8,128)(2,1)} custom-call(bf16[1024,1024]{1,0:T(8,128)(2,1)} %get-tuple-element.80.left_ref, bf16[3,1024,1024]{2,1,0:T(8,128)(2,1)} %get-tuple-element.70.dp_ref.right_ref), custom_call_target="tpu_custom_call" | custom-call | bytes 16777216 | tf_op jit(solution)/shard_map/wqkv/pallas_call | solution.py:305
  364.6 14.5 %wup.1 = bf16[1024,4096]{1,0:T(8,128)(2,1)} custom-call(bf16[1024,1024]{1,0:T(8,128)(2,1)} %get-tuple-element.58.act_ref.left_ref, bf16[1024,4096]{1,0:T(8,128)(2,1)} %get-tuple-element.66.dh_ref.right_ref), custom_call_target="tpu_custom_call" | custom-call | bytes 20971520 | tf_op jit(solution)/shard_map/wup/pallas_call | solution.py:305
  379.1 14.4 %wdown.1 = bf16[4096,1024]{1,0:T(8,128)(2,1)} custom-call(bf16[1024,4096]{1,0:T(8,128)(2,1)} %get-tuple-element.60.act_ref.left_ref, bf16[1024,1024]{1,0:T(8,128)(2,1)} %get-tuple-element.64.dbr_ref.right_ref), custom_call_target="tpu_custom_call" | custom-call | bytes 20971520 | tf_op jit(solution)/shard_map/wdown/pallas_call | solution.py:305
  393.6 0.5 broadcast.165
  394.1 0.7 reduce.8
  394.8 0.7 reduce.7
  395.6 0.7 copy.60
  396.3 17.1 %dact1.1 = (bf16[1024,1024]{1,0:T(8,128)(2,1)}, f32[4,2,1024]{2,1,0:T(2,128)}) custom-call(bf16[3,1024,1024]{2,1,0:T(8,128)(2,1)} %get-tuple-element.70.dp_ref.right_ref, bf16[1024,3072]{1,0:T(8,128)(2,1)} %bitcast.60, bf16[1024,1024]{1,0:T(8,128)(2,1)} %x_ref.5, f32[1024,1024]{1,0:T(8,128)} %get-tuple-element.71.dmid_ref, ...), custom_call_target="tpu_custom_call" | custom-call | bytes 37945344 | tf_op jit(solution)/shard_map/dact1/pallas_call | solution.py:305
  413.4 0.8 convert.22
  414.4 0.7 convert_element_type.86.refs_0_
  415.0 150.5 %reduce.9 = (bf16[2,2,4,2,16,1536]{5,4,3,2,1,0:T(8,128)(2,1)}, f32[8,128]{1,0:T(8,128)}, f32[128,1024]{1,0:T(8,128)}, f32[32,4096]{1,0:T(8,128)}, f32[32,3072]{1,0:T(8,128)}, /*index=5*/f32[32,1024]{1,0:T(8,128)}) custom-call(bf16[16,1536]{1,0:T(8,128)(2,1)} %convert_element_type.86.refs_0_, f32[2,2,4,2,8,128]{5,4,3,2,1,0:T(8,128)} %bitcast.64, ...), custom_call_target="tpu_custom_call" | custom-call | tf_op jit(solution)/shard_map/reduce/pallas_call | solution.py:608
  565.5 2.8 reshape_reshape.19
  568.3 0.6 fusion
  569.0 1.0 fusion.1
  570.0 1.2 fusion.17
  571.2 0.7 convert_reduce_fusion
  571.9 1.3 fusion.22
  573.2 1.2 slice.69
  574.4 1.2 slice_bitcast_fusion
  575.6 0.7 copy.77
  576.3 0.7 copy.78
  577.0 0.8 copy.79
  577.8 0.8 copy.80
  (92 shorter events, 0.9 us)
Async XLA Ops:
  0.6 61.5 %copy-start = (bf16[32,6144]{1,0:T(8,128)(2,1)S(1)}, bf16[32,6144]{1,0:T(8,128)(2,1)}, u32[]{:S(2)}) copy-start(bf16[32,6144]{1,0:T(8,128)(2,1)} %param.21) | copy-start | bytes 1179652
  1.6 1.6 copy-start.22
  2.5 0.7 copy-start.24
  2.5 1.3 copy-start.9
  3.2 0.6 copy-start.11
  4.0 2.2 copy-start.32
  4.0 2.2 copy-start.26
  4.0 2.2 copy-start.27
  4.0 2.2 copy-start.28
  4.0 2.2 copy-start.29
  4.0 2.2 copy-start.30
  4.1 57.7 %copy-start.31 = (bf16[32,1000]{1,0:T(8,128)(2,1)S(1)}, bf16[32,1000]{1,0:T(8,128)(2,1)}, u32[]{:S(2)}) copy-start(bf16[32,1000]{1,0:T(8,128)(2,1)} %param.31) | copy-start | bytes 192004
  60.6 0.7 copy-start.4
  61.3 0.5 copy-start.20
  65.2 108.3 %copy-start.5 = (f32[4,8,8,128]{3,1,2,0:T(8,128)S(1)}, f32[4,8,8,128]{3,1,2,0:T(8,128)}, u32[]{:S(2)}) copy-start(f32[4,8,8,128]{3,1,2,0:T(8,128)} %copy-done.4) | copy-start | bytes 393220
  175.1 12.5 %copy-start.23 = (s32[4]{0:T(128)S(1)}, s32[4]{0:T(128)}, u32[]{:S(2)}) copy-start(s32[4]{0:T(128)} %copy-done.22) | copy-start | bytes 52
  175.1 12.5 %copy-start.25 = (s32[4]{0:T(128)S(1)}, s32[4]{0:T(128)}, u32[]{:S(2)}) copy-start(s32[4]{0:T(128)} %copy-done.24) | copy-start | bytes 52
  175.1 12.6 %copy-start.17 = (s32[1024]{0:T(1024)S(1)}, s32[1024]{0:T(1024)}, u32[]{:S(2)}) copy-start(s32[1024]{0:T(1024)} %param.20) | copy-start | bytes 12292
  175.1 12.7 %copy-start.12 = (s32[1024]{0:T(1024)S(1)}, s32[1024]{0:T(1024)}, u32[]{:S(2)}) copy-start(s32[1024]{0:T(1024)} %copy-done.11) | copy-start | bytes 12292
  175.1 12.7 %copy-start.13 = (s32[1024]{0:T(1024)S(1)}, s32[1024]{0:T(1024)}, u32[]{:S(2)}) copy-start(s32[1024]{0:T(1024)} %get-tuple-element.87) | copy-start | bytes 12292
  175.1 14.2 %copy-start.10 = (s32[1024]{0:T(1024)S(1)}, s32[1024]{0:T(1024)}, u32[]{:S(2)}) copy-start(s32[1024]{0:T(1024)} %copy-done.9) | copy-start | bytes 12292
  305.4 6.0 %copy-start.1 = (bf16[1024,1024]{1,0:T(8,128)(2,1)S(1)}, bf16[1024,1024]{1,0:T(8,128)(2,1)}, u32[]{:S(2)}) copy-start(bf16[1024,1024]{1,0:T(8,128)(2,1)} %get-tuple-element.68.right_ref) | copy-start | bytes 6291460
  379.1 14.4 %copy-start.15 = (f32[8,3,128]{2,1,0:T(4,128)S(1)}, f32[8,3,128]{2,1,0:T(4,128)}, u32[]{:S(2)}) copy-start(f32[8,3,128]{2,1,0:T(4,128)} %get-tuple-element.76) | copy-start | bytes 36868
  379.1 15.0 %copy-start.19 = (f32[1,1024]{1,0:T(1,128)S(1)}, f32[1,1024]{1,0:T(1,128)}, u32[]{:S(2)}) copy-start(f32[1,1024]{1,0:T(1,128)} %get-tuple-element.77) | copy-start | bytes 12292
  379.1 15.7 %copy-start.18 = (f32[1,1024]{1,0:T(1,128)S(1)}, f32[1,1024]{1,0:T(1,128)}, u32[]{:S(2)}) copy-start(f32[1,1024]{1,0:T(1,128)} %get-tuple-element.79) | copy-start | bytes 12292
  379.1 16.5 %copy-start.14 = (f32[1,4096]{1,0:T(1,128)S(1)}, f32[1,4096]{1,0:T(1,128)}, u32[]{:S(2)}) copy-start(f32[1,4096]{1,0:T(1,128)} %get-tuple-element.78) | copy-start | bytes 49156
  396.3 17.9 %copy-start.8 = (f32[4,3,1024]{2,1,0:T(4,128)S(1)}, f32[4,3,1024]{2,1,0:T(4,128)}, u32[]{:S(2)}) copy-start(f32[4,3,1024]{2,1,0:T(4,128)} %get-tuple-element.74) | copy-start | bytes 147460
  396.3 18.0 %copy-start.16 = (f32[4,1024]{1,0:T(4,128)S(1)}, f32[4,1024]{1,0:T(4,128)}, u32[]{:S(2)}) copy-start(f32[4,1024]{1,0:T(4,128)} %get-tuple-element.75) | copy-start | bytes 49156
  565.5 3.4 copy-start.21
  568.3 7.3 %copy-start.6 = (f32[32,3072]{1,0:T(8,128)S(1)}, f32[32,3072]{1,0:T(8,128)}, u32[]{:S(2)}) copy-start(f32[32,3072]{1,0:T(8,128)} %get-tuple-element.123) | copy-start | bytes 1179652
  568.9 7.4 %copy-start.7 = (f32[32,1024]{1,0:T(8,128)S(1)}, f32[32,1024]{1,0:T(8,128)}, u32[]{:S(2)}) copy-start(f32[32,1024]{1,0:T(8,128)} %get-tuple-element.125) | copy-start | bytes 393220
  568.9 8.0 %copy-start.3 = (f32[32,4096]{1,0:T(8,128)S(1)}, f32[32,4096]{1,0:T(8,128)}, u32[]{:S(2)}) copy-start(f32[32,4096]{1,0:T(8,128)} %get-tuple-element.127) | copy-start | bytes 1572868
  570.0 7.8 %copy-start.2 = (f32[128,1024]{1,0:T(8,128)S(1)}, f32[128,1024]{1,0:T(8,128)}, u32[]{:S(2)}) copy-start(f32[128,1024]{1,0:T(8,128)} %get-tuple-element.129) | copy-start | bytes 1572868
